TPU v7x, 32 devices: a whole 2x2x4 slice. The times are simulated.
32 devices in a mesh: section: 2 (over core), dp: 16 (over z, y, x).
Axes of the slice: x: 2, y: 2, z: 4, core: 2. Of those that a mesh axis runs over, the one named last changes fastest.
Arguments:
- entry_pair: bfloat16 [2, 32, 256, 1024], P('section', 'dp'), may hold values from -6 to 6
- paragraph_labels: int32 [32, 256], P('dp'), may hold values from 0 to 1, never falling along the last dimension, each value on 1 to 192 neighbouring positions
- initial_norm_scaling: bfloat16 [2, 1024], P('section'), may hold values from 0.5 to 1.5
- initial_norm_offset: bfloat16 [2, 1024], P('section'), may hold values from -2 to 2
- log_fading_rates: bfloat16 [2, 1024], P('section'), may hold values from -8 to -2
- present_position_reward: bfloat16 [2, 1024], P('section'), may hold values from -1 to 1
- shift_ratio_lookup: bfloat16 [2, 1024], P('section'), may hold values from 0 to 1
- shift_ratio_content: bfloat16 [2, 1024], P('section'), may hold values from 0 to 1
- shift_ratio_accept: bfloat16 [2, 1024], P('section'), may hold values from 0 to 1
- attention_lookup_matrix: bfloat16 [2, 1024, 1024], P('section'), may hold values from -0.1875 to 0.1875
- attention_content_matrix: bfloat16 [2, 1024, 1024], P('section'), may hold values from -0.1875 to 0.1875
- attention_accept_matrix: bfloat16 [2, 1024, 1024], P('section'), may hold values from -0.1875 to 0.1875
- attention_exit_matrix: bfloat16 [2, 1024, 1024], P('section'), may hold values from -0.75 to 0.75
- latter_norm_scaling: bfloat16 [2, 1024], P('section'), may hold values from 0.5 to 1.5
- latter_norm_offset: bfloat16 [2, 1024], P('section'), may hold values from -2 to 2
- feedforward_lookup_ratio: bfloat16 [2, 1024], P('section'), may hold values from 0 to 1
- feedforward_accept_ratio: bfloat16 [2, 1024], P('section'), may hold values from 0 to 1
- feedforward_lookup_matrix: bfloat16 [2, 1024, 4096], P('section'), may hold values from -0.1875 to 0.1875
- feedforward_accept_matrix: bfloat16 [2, 1024, 1024], P('section'), may hold values from -0.1875 to 0.1875
- feedforward_content_matrix: bfloat16 [2, 4096, 1024], P('section'), may hold values from -0.09375 to 0.09375
Outputs:
- block_ends: float32 [2, 32, 256, 1024], P('section', 'dp')
- first_gain_gradient: float32 [2, 1024], P('section', 'dp')
- first_bias_gradient: float32 [2, 1024], P('section', 'dp')
- time_decay_gradient: float32 [2, 1024], P('section', 'dp')
- time_first_gradient: float32 [2, 1024], P('section', 'dp')
- blend_key_gradient: float32 [2, 1024], P('section', 'dp')
- blend_value_gradient: float32 [2, 1024], P('section', 'dp')
- blend_recept_gradient: float32 [2, 1024], P('section', 'dp')
- weight_key_gradient: float32 [2, 1024, 1024], P('section', 'dp')
- weight_value_gradient: float32 [2, 1024, 1024], P('section', 'dp')
- weight_recept_gradient: float32 [2, 1024, 1024], P('section', 'dp')
- weight_output_gradient: float32 [2, 1024, 1024], P('section', 'dp')
- second_gain_gradient: float32 [2, 1024], P('section', 'dp')
- second_bias_gradient: float32 [2, 1024], P('section', 'dp')
- channel_key_gradient: float32 [2, 1024], P('section', 'dp')
- channel_recept_gradient: float32 [2, 1024], P('section', 'dp')
- hidden_key_gradient: float32 [2, 1024, 4096], P('section', 'dp')
- hidden_recept_gradient: float32 [2, 1024, 1024], P('section', 'dp')
- hidden_value_gradient: float32 [2, 4096, 1024], P('section', 'dp')
Inputs may be any that keep to these rules, and one draw needn't show every extreme that they name: `paragraph_labels`: in every row the document number is 0 up to some token and 1 from there on, so a row holds two documents, each of 64 to 192 tokens.
All inputs are finite; a program needn't handle non-finite values.
Results may differ from a plain program's by a relative error of at most 0.015.
Values may be sent and summed in bfloat16 or wider, within the bound.
No kernel may reach another device: no remote copies, remote signals or barrier semaphores. Data moves between devices by JAX's collectives and lax.ppermute only.
A program may use at most 256 MiB of HBM per device.

v0:
```python
import functools

import jax
import jax.numpy as jnp
from jax import lax
from jax.experimental import pallas as pl
from jax.experimental.pallas import tpu as pltpu
from jax.sharding import PartitionSpec as P

BF = jnp.bfloat16
F32 = jnp.float32
LANES = 128
VM = pl.BlockSpec(memory_space=pltpu.VMEM)
HBM = pl.BlockSpec(memory_space=pl.ANY)
SM = pl.BlockSpec(memory_space=pltpu.SMEM)

def dot(left, right):
    return jnp.dot(left, right, preferred_element_type=F32)

def dot_nt(left, right):
    return lax.dot_general(left, right, (((1,), (1,)), ((), ())), preferred_element_type=F32)

def lanes(c):
    return pl.ds(pl.multiple_of(c * LANES, LANES), LANES)

def slabs(vector, scratch):
    for c in range(scratch.shape[0]):
        scratch[c:c + 1, :] = vector[:, c * LANES:(c + 1) * LANES].astype(F32)
    return scratch[...]

def statistics(source, mean, scale, tokens, width, chunk=128):
    def step(i, _):
        at = pl.ds(pl.multiple_of(i * chunk, chunk), chunk)
        x = source[at, :].astype(F32)
        m = jnp.sum(x, axis=1, keepdims=True) * (1.0 / width)
        x = x - m
        v = jnp.sum(x * x, axis=1, keepdims=True) * (1.0 / width)
        mean[at, :] = jnp.broadcast_to(m, (chunk, LANES))
        scale[at, :] = jnp.broadcast_to(lax.rsqrt(v + 1e-05), (chunk, LANES))
        return 0
    lax.fori_loop(0, tokens // chunk, step, 0)

def mix_into(source, mean, scale, same, gain, bias, factors, targets, width):
    def step(c, _):
        cols = lanes(c)
        z = (source[:, cols].astype(F32) - mean[...]) * scale[...] * gain[:, cols].astype(F32) + bias[:, cols].astype(F32)
        before = pltpu.roll(z, 1, 0) * same[...]
        step_up = z - before
        for factor, target in zip(factors, targets):
            target[:, cols] = (before + step_up * factor[:, cols].astype(F32)).astype(BF)
        return 0
    lax.fori_loop(0, width // LANES, step, 0)

def fetch(pairs, sems):
    copies = [pltpu.make_async_copy(s, d, sems.at[i]) for i, (s, d) in enumerate(pairs)]
    for c in copies:
        c.start()
    return copies

def forward_kernel(rows, with_delta, orders, *refs):
    if orders:
        bits, refs = refs[0], refs[1:]
    (same_s, same, h, g1, b1, fade, bonus, mk, mv, mr, g2, b2, ck, cr, cot) = refs[:15]
    weights = refs[15:22]
    n_out = 20
    outs = refs[22:22 + n_out]
    if orders:
        pieces, piece_sems, refs = refs[22 + n_out:26 + n_out], refs[-1], refs[:22 + n_out] + refs[26 + n_out:-1]
    (wk, wv, wr, wo, fk, fr, fv, mean, scale, mean2, scale2, key_in, value_in, recept_in, ks, vs, ys, tops, bottoms, gate, mixed, middle,
     hidden_in, gate_in, act, slab, in_sems, out_sems) = refs[22 + n_out:]
    tokens, width = h.shape
    each = tokens // rows
    parts = width // LANES
    tile = 512
    large = 1024
    ff = act.shape[1]
    loads = fetch(list(zip(weights, (wk, wv, wr, wo, fk, fr, fv))), in_sems)
    saves = []

    def save(source):
        i = len(saves)
        saves.append(pltpu.make_async_copy(source, outs[i], out_sems.at[i]))
        saves[-1].start()

    statistics(h, mean, scale, tokens, width)
    mix_into(h, mean, scale, same, g1, b1, (mk, mv, mr), (key_in, value_in, recept_in), width)
    for z in (key_in, value_in, recept_in):
        save(z)

    def cols_of(j):
        return pl.ds(pl.multiple_of(j * tile, tile), tile)

    def steps_tile(values, target, j):
        for row in range(rows):
            for c in range(tile // LANES):
                target[pl.ds(row * each * parts + j * (tile // LANES) + c, each, stride=parts), :] = values[row * each:(row + 1) * each, c * LANES:(c + 1) * LANES]

    loads[0].wait()
    def key_tile(j, _):
        steps_tile(dot(key_in[...], wk[:, cols_of(j)]), ks, j)
        return 0
    lax.fori_loop(0, width // tile, key_tile, 0)
    loads[1].wait()
    def value_tile(j, _):
        steps_tile(dot(value_in[...], wv[:, cols_of(j)]), vs, j)
        return 0
    lax.fori_loop(0, width // tile, value_tile, 0)
    save(ks)
    save(vs)
    loads[2].wait()
    def accept_tile(j, _):
        gate[:, cols_of(j)] = jax.nn.sigmoid(dot(recept_in[...], wr[:, cols_of(j)]))
        return 0
    lax.fori_loop(0, width // tile, accept_tile, 0)
    save(gate)

    decay = jnp.exp(-jnp.exp(slabs(fade, slab)))
    extra = slabs(bonus, slab)
    def step(t, carry):
        following = []
        for row in range(rows):
            here = pl.ds(pl.multiple_of((row * each + t) * parts, parts), parts)
            m = same_s[row, t]
            top, bottom = carry[2 * row] * m, carry[2 * row + 1] * m
            tops[here, :] = top
            bottoms[here, :] = bottom
            k, v = ks[here, :], vs[here, :]
            ek, now = jnp.exp(k), jnp.exp(extra + k)
            ys[here, :] = (top + now * v) / (bottom + now)
            following += [decay * top + ek * v, decay * bottom + ek]
        return tuple(following)
    zero = jnp.zeros(decay.shape, F32)
    lax.fori_loop(0, each, step, (zero,) * (2 * rows), unroll=4)
    save(tops)
    save(bottoms)

    for row in range(rows):
        def mixed_step(c, _, row=row):
            y = ys[pl.ds(row * each * parts + c, each, stride=parts), :]
            mixed[row * each:(row + 1) * each, lanes(c)] = (gate[row * each:(row + 1) * each, lanes(c)] * y).astype(BF)
            return 0
        lax.fori_loop(0, parts, mixed_step, 0)
    save(mixed)
    loads[3].wait()
    def middle_tile(j, _):
        middle[:, cols_of(j)] = h[:, cols_of(j)].astype(F32) + dot(mixed[...], wo[:, cols_of(j)])
        return 0
    lax.fori_loop(0, width // tile, middle_tile, 0)
    save(middle)

    statistics(middle, mean2, scale2, tokens, width)
    mix_into(middle, mean2, scale2, same, g2, b2, (ck, cr), (hidden_in, gate_in), width)
    save(hidden_in)
    save(gate_in)
    loads[4].wait()
    def hidden_tile(j, _):
        cols = pl.ds(pl.multiple_of(j * large, large), large)
        r = jnp.maximum(dot(hidden_in[...], fk[:, cols]), 0.0)
        act[:, cols] = (r * r).astype(BF)
        return 0
    lax.fori_loop(0, ff // large, hidden_tile, 0)
    save(act)
    piece_waits = []
    if orders:
        share = ff // 16
        for d in range(16):
            first, one, two = orders[d >> 3][:3]
            source = act.at[:, d * share:(d + 1) * share]
            column = (((d >> one) & 1) * 2 + ((d >> two) & 1)) * share
            relative = ((d >> first) & 1) ^ bits[first]
            for r, target in ((1, pieces[2 * (d >> 3)]), (0, pieces[2 * (d >> 3) + 1])):
                copy = pltpu.make_async_copy(source, target.at[:, column:column + share], piece_sems.at[d])
                @pl.when(relative == r)
                def _(copy=copy):
                    copy.start()
            piece_waits.append(copy)
    for i in (0, 1, 2, 5):
        saves[i].wait()
    result, delta_out, delta_gate = key_in, value_in, recept_in
    loads[5].wait()
    def gate_tile(j, _):
        gate[:, cols_of(j)] = jax.nn.sigmoid(dot(gate_in[...], fr[:, cols_of(j)]))
        return 0
    lax.fori_loop(0, width // tile, gate_tile, 0)
    loads[6].wait()
    def out_tile(j, _):
        cols = cols_of(j)
        o = dot(act[...], fv[:, cols])
        s = gate[:, cols]
        result[:, cols] = (middle[:, cols] + s * o).astype(BF)
        g = cot[:, cols].astype(F32)
        if with_delta:
            delta_out[:, cols] = (g * s).astype(BF)
            delta_gate[:, cols] = (g * o * s * (1.0 - s)).astype(BF)
        else:
            delta_out[:, cols] = s.astype(BF)
            delta_gate[:, cols] = (o * s * (1.0 - s)).astype(BF)
        return 0
    lax.fori_loop(0, width // tile, out_tile, 0)
    save(result)
    save(delta_out)
    save(delta_gate)
    for z in (mean, scale, mean2, scale2):
        save(z)
    if orders and with_delta:
        for i in (0, 1):
            piece_waits.append(pltpu.make_async_copy(delta_out, pieces[2 * i].at[:, width:2 * width], piece_sems.at[16 + i]))
            piece_waits[-1].start()
    for copy in piece_waits:
        copy.wait()
    for i, c in enumerate(saves):
        if i not in (0, 1, 2, 5):
            c.wait()

def forward(rows, with_delta, same_s, same, h, p, cot, bits=None, orders=None):
    (g1, b1, fade, bonus, mk, mv, mr, wk, wv, wr, wo, g2, b2, ck, cr, fk, fr, fv) = p
    tokens, width = h.shape
    ff = fk.shape[1]
    vm = pl.BlockSpec(memory_space=pltpu.VMEM)
    hbm = pl.BlockSpec(memory_space=pl.ANY)
    slabs = tokens * width // LANES
    outs = [((tokens, width), BF)] * 3 + [((slabs, LANES), F32)] * 2 + [((tokens, width), F32)] + [((slabs, LANES), F32)] * 2
    outs += [((tokens, width), BF), ((tokens, width), F32)]
    outs += [((tokens, width), BF)] * 2 + [((tokens, ff), BF)] + [((tokens, width), BF)] * 3
    outs = outs[:14] if False else outs
    outs += [((tokens, LANES), F32)] * 4
    wide, wide32, step32 = pltpu.VMEM((tokens, width), BF), pltpu.VMEM((tokens, width), F32), pltpu.VMEM((slabs, LANES), F32)
    stat = pltpu.VMEM((tokens, LANES), F32)
    square = pltpu.VMEM((width, width), BF)
    big = pltpu.VMEM((tokens, ff), BF)
    scratch = [square] * 4 + [pltpu.VMEM((width, ff), BF), square, pltpu.VMEM((ff, width), BF), stat, stat, stat, stat] + [wide] * 3
    scratch += [step32] * 5 + [wide32, wide, wide32, wide, wide, big]
    scratch += [pltpu.VMEM((width // LANES, LANES), F32), pltpu.SemaphoreType.DMA((7,)), pltpu.SemaphoreType.DMA((len(outs),))]
    if orders:
        sent = (tokens, width * (1 + with_delta))
        outs += [(sent, BF), ((tokens, width), BF)] * 2
        scratch.append(pltpu.SemaphoreType.DMA((18,)))
    smem = pl.BlockSpec(memory_space=pltpu.SMEM)
    return pl.pallas_call(
        functools.partial(forward_kernel, rows, with_delta, orders),
        out_shape=tuple(jax.ShapeDtypeStruct(*o) for o in outs),
        in_specs=[smem] * (orders is not None) + [smem] + [vm] * 14 + [hbm] * 7,
        out_specs=(hbm,) * len(outs),
        scratch_shapes=scratch,
        compiler_params=pltpu.CompilerParams(vmem_limit_bytes=60 << 20),
        cost_estimate=pl.CostEstimate(flops=90000000000, bytes_accessed=261000000, transcendentals=0),
        name="forward",
    )(*([bits] if orders else []), same_s, same, h, g1, b1, fade, bonus, mk, mv, mr, g2, b2, ck, cr, cot, wk, wv, wr, wo, fk, fr, fv)

def norm_backward(source, mean, scale, same, gain, bias, factors, grads, residual, targets, sums, hats, first, second, rows, leave):
    tokens, width = source.shape
    each = tokens // rows
    spans = [slice(row * each, (row + 1) * each) for row in range(rows)]

    def gather(c, carry):
        cols = lanes(c)
        g, b = gain[:, cols].astype(F32), bias[:, cols].astype(F32)
        following = []
        totals = [0.0] * (2 + len(grads))
        for row, at in enumerate(spans):
            hat = (source[at, cols].astype(F32) - mean[at, :]) * scale[at, :]
            z = hat * g + b
            step_up = z - pltpu.roll(z, 1, 0) * same[at, :]
            straight = rest = None
            for i, (factor, grad) in enumerate(zip(factors, grads)):
                d = grad[at, cols]
                df = d * factor[:, cols].astype(F32)
                totals[2 + i] += jnp.sum(d * step_up, axis=0, keepdims=True)
                straight = df if i == 0 else straight + df
                rest = d - df if i == 0 else rest + (d - df)
            dz = straight + pltpu.roll(rest * same[at, :], each - 1, 0)
            totals[0] += jnp.sum(dz * hat, axis=0, keepdims=True)
            totals[1] += jnp.sum(dz, axis=0, keepdims=True)
            dhat = dz * g
            hats[at, cols] = dhat
            following += [carry[2 * row] + dhat, carry[2 * row + 1] + dhat * hat]
        for i, total in enumerate(totals):
            sums[i:i + 1, cols] = total
        return tuple(following)

    zero = jnp.zeros((each, LANES), F32)
    done = lax.fori_loop(0, width // LANES, gather, (zero,) * (2 * rows))
    for row, at in enumerate(spans):
        for ref, value in ((first, done[2 * row]), (second, done[2 * row + 1])):
            ref[at, :] = jnp.broadcast_to(jnp.sum(value, axis=1, keepdims=True) * (1.0 / width), (each, LANES))

    for at in spans:
        def finish(c, _, at=at):
            cols = lanes(c)
            hat = (source[at, cols].astype(F32) - mean[at, :]) * scale[at, :]
            out = residual[at, cols].astype(F32) + scale[at, :] * (hats[at, cols] - first[at, :] - hat * second[at, :])
            for t in targets:
                t[at, cols] = out.astype(t.dtype)
            return 0

        lax.fori_loop(0, width // LANES, finish, 0)
        leave(at)


def channel_kernel(rows, times, *refs):
    (same, factor_out, factor_gate, g, g2, b2, ck, cr, rect_in, middle_in, mean_in, scale_in, fv_in, fk_in, fr_in) = refs[:15]
    n_out = 6
    outs = refs[15:15 + n_out]
    (fv, fk, fr, rect, middle, delta_out, delta_gate, delta_pre, dh, dg, mean, scale, first, second, hats, delta, branch, sums, in_sems, out_sems, row_sems) = refs[15 + n_out:]
    tokens, width = g.shape
    ff = rect.shape[1]
    tile = 512
    chunks = ff // tile
    first_loads = []
    for j in range(chunks):
        span = slice(j * tile, (j + 1) * tile)
        first_loads += [(fv_in.at[span, :], fv.at[span, :]), (rect_in.at[:, span], rect.at[:, span])]
    sums[...] = jnp.zeros_like(sums)
    loads = fetch(first_loads + [(fr_in, fr), (fk_in, fk), (middle_in, middle), (mean_in, mean), (scale_in, scale)], in_sems)
    saves = []
    def save(source, i):
        saves.append(pltpu.make_async_copy(source, outs[i], out_sems.at[i]))
        saves[-1].start()
    def cols_of(j):
        return pl.ds(pl.multiple_of(j * tile, tile), tile)
    if times:
        def scale_tile(j, _):
            cols = lanes(j)
            x = g[:, cols].astype(F32)
            delta_out[:, cols] = (x * factor_out[:, cols].astype(F32)).astype(BF)
            delta_gate[:, cols] = (x * factor_gate[:, cols].astype(F32)).astype(BF)
            return 0
        lax.fori_loop(0, width // LANES, scale_tile, 0)
        left_out, left_gate = delta_out, delta_gate
    else:
        left_out, left_gate = factor_out, factor_gate
    def pre_tile(j, _):
        cols = cols_of(j)
        pltpu.make_async_copy(fv_in.at[cols, :], fv.at[cols, :], in_sems.at[2 * j]).wait()
        pltpu.make_async_copy(rect_in.at[:, cols], rect.at[:, cols], in_sems.at[2 * j + 1]).wait()
        d = dot_nt(left_out[...], fv[cols, :])
        delta_pre[:, cols] = (d * (2.0 * jnp.sqrt(rect[:, cols].astype(F32)))).astype(BF)
        return 0
    lax.fori_loop(0, ff // tile, pre_tile, 0)
    save(delta_pre, 0)
    if times:
        save(delta_out, 4)
        save(delta_gate, 5)
    for c in loads[-5:]:
        c.wait()
    def hidden_tile(j, _):
        cols = cols_of(j)
        dh[:, cols] = dot_nt(delta_pre[...], fk[cols, :])
        dg[:, cols] = dot_nt(left_gate[...], fr[cols, :])
        return 0
    lax.fori_loop(0, width // tile, hidden_tile, 0)
    def leave(at):
        for i, z in ((1, delta), (2, branch)):
            saves.append(pltpu.make_async_copy(z.at[at, :], outs[i].at[at, :], row_sems.at[i - 1, at.start // (tokens // rows)]))
            saves[-1].start()
    norm_backward(middle, mean, scale, same, g2, b2, (ck, cr), (dh, dg), g, (delta, branch), sums, hats, first, second, rows, leave)
    save(sums, 3)
    for c in saves:
        c.wait()

def channel(rows, times, same, factor_out, factor_gate, g, p, rect, middle, mean, scale):
    (g1, b1, fade, bonus, mk, mv, mr, wk, wv, wr, wo, g2, b2, ck, cr, fk, fr, fv) = p
    tokens, width = g.shape
    ff = fk.shape[1]
    vm = pl.BlockSpec(memory_space=pltpu.VMEM)
    hbm = pl.BlockSpec(memory_space=pl.ANY)
    outs = [((tokens, ff), BF), ((tokens, width), F32), ((tokens, width), BF), ((8, width), F32)]
    outs += [((tokens, width), BF)] * 2 if times else [((16, LANES), BF)] * 2
    wide, wide32 = pltpu.VMEM((tokens, width), BF), pltpu.VMEM((tokens, width), F32)
    stat = pltpu.VMEM((tokens, LANES), F32)
    big = pltpu.VMEM((tokens, ff), BF)
    scratch = [pltpu.VMEM((ff, width), BF), pltpu.VMEM((width, ff), BF), pltpu.VMEM((width, width), BF), big, wide32, wide, wide, big, wide32, wide32]
    scratch += [stat] * 4 + [wide32, wide32, wide, pltpu.VMEM((8, width), F32), pltpu.SemaphoreType.DMA((2 * ff // 512 + 5,)), pltpu.SemaphoreType.DMA((6,)), pltpu.SemaphoreType.DMA((2, rows))]
    return pl.pallas_call(
        functools.partial(channel_kernel, rows, times),
        out_shape=tuple(jax.ShapeDtypeStruct(*o) for o in outs),
        in_specs=[vm] * 8 + [hbm] * 7,
        out_specs=(hbm,) * 6,
        scratch_shapes=scratch,
        compiler_params=pltpu.CompilerParams(vmem_limit_bytes=60 << 20),
        cost_estimate=pl.CostEstimate(flops=75000000000, bytes_accessed=217500000, transcendentals=0),
        name="channel",
    )(same, factor_out, factor_gate, g, g2, b2, ck, cr, rect, middle, mean, scale, fv, fk, fr)

def time_kernel(rows, *refs):
    (same_s, same, branch, h, g1, b1, fade, bonus, mk, mv, mr, wo_in, gate_in, ks_in, vs_in, tops_in, bottoms_in, wk_in, wv_in, wr_in, delta_in, mean_in, scale_in) = refs[:23]
    n_out = 5
    outs = refs[23:23 + n_out]
    (wo, gate, ks, vs, wk, wv, wr, delta, dm, gs, ys, tops, bottoms, dks, dvs, dk, dv, dr, ik, iv, ir, mean, scale, first, second, hats, state, sums, slab, in_sems, out_sems, row_sems) = refs[23 + n_out:]
    tokens, width = h.shape
    each = tokens // rows
    parts = width // LANES
    tile = 512
    sums[...] = jnp.zeros_like(sums)
    loads = fetch([(wo_in, wo), (gate_in, gate), (ks_in, ks), (vs_in, vs), (tops_in, tops), (bottoms_in, bottoms), (wk_in, wk), (wv_in, wv), (wr_in, wr), (delta_in, delta), (mean_in, mean), (scale_in, scale)], in_sems)
    saves = []
    def save(source, i):
        saves.append(pltpu.make_async_copy(source, outs[i], out_sems.at[i]))
        saves[-1].start()
    def cols_of(j):
        return pl.ds(pl.multiple_of(j * tile, tile), tile)
    loads[0].wait()
    loads[1].wait()
    def mixed_tile(j, _):
        cols = cols_of(j)
        d = dot_nt(branch[...], wo[cols, :])
        dm[:, cols] = d
        e = d * gate[:, cols]
        for row in range(rows):
            for c in range(tile // LANES):
                gs[pl.ds(row * each * parts + j * (tile // LANES) + c, each, stride=parts), :] = e[row * each:(row + 1) * each, c * LANES:(c + 1) * LANES]
        return 0
    lax.fori_loop(0, width // tile, mixed_tile, 0)
    for i in (2, 3, 4, 5):
        loads[i].wait()
    rate = jnp.exp(slabs(fade, slab))
    decay = jnp.exp(-rate)
    extra = slabs(bonus, slab)
    zero = jnp.zeros(decay.shape, F32)
    def back(i, carry):
        t = each - 1 - i
        dw, du = carry[:2]
        following = []
        for row in range(rows):
            here = pl.ds(pl.multiple_of((row * each + t) * parts, parts), parts)
            a, b = carry[2 + 2 * row], carry[3 + 2 * row]
            k, v = ks[here, :], vs[here, :]
            ek, now = jnp.exp(k), jnp.exp(extra + k)
            inverse = 1.0 / (bottoms[here, :] + now)
            y = (tops[here, :] + now * v) * inverse
            ys[here, :] = y
            ga = gs[here, :] * inverse
            gb = -ga * y
            q = now * (v * ga + gb)
            dks[here, :] = ek * (v * a + b) + q
            dvs[here, :] = ek * a + now * ga
            du = du + q
            dw = dw + (a * tops[here, :] + b * bottoms[here, :])
            m = same_s[row, t]
            following += [(ga + decay * a) * m, (gb + decay * b) * m]
        return (dw, du, *following)
    done = lax.fori_loop(0, each, back, (zero,) * (2 + 2 * rows), unroll=4)
    dfade = -done[0] * decay * rate
    for c in range(parts):
        sums[5:6, c * LANES:(c + 1) * LANES] = dfade[c:c + 1, :]
        sums[6:7, c * LANES:(c + 1) * LANES] = done[1][c:c + 1, :]
    for row in range(rows):
        def out_step(c, _, row=row):
            span = slice(row * each, (row + 1) * each)
            cols = lanes(c)
            at = pl.ds(row * each * parts + c, each, stride=parts)
            dk[span, cols] = dks[at, :].astype(BF)
            dv[span, cols] = dvs[at, :].astype(BF)
            s = gate[span, cols]
            dr[span, cols] = (dm[span, cols] * ys[at, :] * s * (1.0 - s)).astype(BF)
            return 0
        lax.fori_loop(0, parts, out_step, 0)
    for i, z in enumerate((dk, dv, dr)):
        save(z, i)
    for i in (6, 7, 8):
        loads[i].wait()
    def in_tile(j, _):
        cols = cols_of(j)
        ik[:, cols] = dot_nt(dk[...], wk[cols, :])
        iv[:, cols] = dot_nt(dv[...], wv[cols, :])
        ir[:, cols] = dot_nt(dr[...], wr[cols, :])
        return 0
    lax.fori_loop(0, width // tile, in_tile, 0)
    for c in loads[9:]:
        c.wait()
    def leave(at):
        saves.append(pltpu.make_async_copy(state.at[at, :], outs[3].at[at, :], row_sems.at[at.start // each]))
        saves[-1].start()
    norm_backward(h, mean, scale, same, g1, b1, (mk, mv, mr), (ik, iv, ir), delta, (state,), sums, hats, first, second, rows, leave)
    save(sums, 4)
    for c in saves:
        c.wait()

def time_mix(rows, dtype, same_s, same, branch, delta, h, p, gate, ks, vs, tops, bottoms, mean, scale):
    (g1, b1, fade, bonus, mk, mv, mr, wk, wv, wr, wo, g2, b2, ck, cr, fk, fr, fv) = p
    tokens, width = h.shape
    vm = pl.BlockSpec(memory_space=pltpu.VMEM)
    hbm = pl.BlockSpec(memory_space=pl.ANY)
    outs = [((tokens, width), BF)] * 3 + [((tokens, width), dtype), ((8, width), F32)]
    wide, wide32 = pltpu.VMEM((tokens, width), BF), pltpu.VMEM((tokens, width), F32)
    step32 = pltpu.VMEM(ks.shape, F32)
    stat = pltpu.VMEM((tokens, LANES), F32)
    square = pltpu.VMEM((width, width), BF)
    scratch = [square, wide32, step32, step32, square, square, square, wide32, wide32] + [step32] * 6 + [wide] * 3 + [wide32] * 3 + [stat] * 4 + [wide32]
    scratch += [pltpu.VMEM((tokens, width), dtype), pltpu.VMEM((8, width), F32), pltpu.VMEM((width // LANES, LANES), F32), pltpu.SemaphoreType.DMA((12,)), pltpu.SemaphoreType.DMA((5,)), pltpu.SemaphoreType.DMA((rows,))]
    return pl.pallas_call(
        functools.partial(time_kernel, rows),
        out_shape=tuple(jax.ShapeDtypeStruct(*o) for o in outs),
        in_specs=[pl.BlockSpec(memory_space=pltpu.SMEM)] + [vm] * 10 + [hbm] * 12,
        out_specs=(hbm,) * 5,
        scratch_shapes=scratch,
        compiler_params=pltpu.CompilerParams(vmem_limit_bytes=60 << 20),
        cost_estimate=pl.CostEstimate(flops=87000000000, bytes_accessed=252300000, transcendentals=0),
        name="time_mix",
    )(same_s, same, branch, h, g1, b1, fade, bonus, mk, mv, mr, wo, gate, ks, vs, tops, bottoms, wk, wv, wr, delta, mean, scale)


UNIT = 1024


def starts(parts):
    return [sum(c for c, _ in parts[:i]) for i in range(len(parts))]


def terms_kernel(count, parts, shapes, with_sums, with_factor, *refs):
    bits, refs = refs[0], refs[1:]
    if with_factor:
        factor, refs = refs[0], refs[1:]
    n, np_ = len(shapes), len(parts)
    left_in, right_in, refs = refs[:n], refs[n:2 * n], refs[2 * n:]
    if with_sums:
        early, late, *refs = refs
    outs, refs = refs[:2 * np_], refs[2 * np_:]
    lefts, rights, refs = refs[:n], refs[n:2 * n], refs[2 * n:]
    bufs, (in_sems, out_sems) = refs[:np_], refs[np_:]
    sends, keeps = outs[::2], outs[1::2]
    tile = 512
    columns = starts(parts)

    def place(order, d):
        bit = [(d >> b) & 1 if isinstance(d, int) else lax.rem(lax.div(d, 1 << b), 2) for b in order]
        return bit[0] ^ bits[order[0]], bit[1] * 4 + bit[2] * 2 + bit[3]

    chunk_base = [sum(kin // tile for kin, _ in shapes[:m]) for m in range(n)]

    def load(m, j):
        cols = pl.ds(pl.multiple_of(j * tile, tile), tile)
        return pltpu.make_async_copy(left_in[m].at[:, cols], lefts[m].at[:, cols], in_sems.at[chunk_base[m] + j])

    right_base = [chunk_base[-1] + shapes[-1][0] // tile + sum(width // UNIT for _, width in shapes[:m]) for m in range(n)]

    def load_right(m, q):
        cols = slice(q * UNIT, (q + 1) * UNIT)
        return pltpu.make_async_copy(right_in[m].at[:, cols], rights[m].at[:, cols], in_sems.at[right_base[m] + q])

    for m, (kin, width) in enumerate(shapes):
        load_right(m, 0).start()
        for j in range(kin // tile):
            load(m, j).start()
        for q in range(1, width // UNIT):
            load_right(m, q).start()
    waits = []
    base = 0
    blocks = 0
    for m, ((kin, width), left, right) in enumerate(zip(shapes, lefts, rights)):
        rows = kin // count
        per = tile // rows
        for q in range(width // UNIT):
            load_right(m, q).wait()
            if with_factor:
                right[...] = (right[...].astype(F32) * factor[...].astype(F32)).astype(BF)

            def step(j, _, m=m, q=q, left=left, right=right, rows=rows, per=per, base=base):
                if q == 0:
                    load(m, j).wait()
                lhs = left[:, pl.ds(pl.multiple_of(j * tile, tile), tile)]
                for i, (cols, order) in enumerate(parts):
                    at = q * UNIT + columns[i]
                    res = lax.dot_general(lhs, right[:, at:at + cols], (((0,), (0,)), ((), ())), preferred_element_type=F32).astype(BF)
                    for s in range(per):
                        relative, index = place(order, j * per + s)
                        bufs[i][relative, index, base:base + rows, :] = res[s * rows:(s + 1) * rows]
                        if rows >= 256:
                            source = bufs[i].at[relative, index]
                            for r, target in ((1, sends[i]), (0, keeps[i])):
                                @pl.when(relative == r)
                                def _(source=source, target=target, index=index, i=i):
                                    pltpu.make_async_copy(source, target.at[index], out_sems.at[i, j * per + s]).start()
                return 0

            lax.fori_loop(0, kin // tile, step, 0)
            for i in range(np_):
                if rows >= 256:
                    for j in range(count):
                        waits.append(pltpu.make_async_copy(bufs[i].at[0, 0], keeps[i].at[0], out_sems.at[i, j]))
                else:
                    for r, target in ((1, sends[i]), (0, keeps[i])):
                        c = pltpu.make_async_copy(bufs[i].at[r, :, base:base + rows, :], target.at[:, base:base + rows, :], out_sems.at[i, 2 * blocks + r])
                        c.start()
                        waits.append(c)
            base += rows
            blocks += 1
    if with_sums:
        share = early.shape[1] // count
        both = jnp.concatenate([early[...], late[...]], axis=0)
        for buf in bufs:
            buf[:, :, base:base + 16, :] = jnp.zeros(buf.shape[:2] + (16, buf.shape[3]), BF)
        for d in range(count):
            column = d * share // LANES * LANES
            piece = both[:, column:column + LANES]
            if d * share - column:
                piece = pltpu.roll(piece, LANES - (d * share - column), 1)
            relative, index = place(parts[0][1], d)
            bufs[0][relative, index, base:base + 16, 0:LANES] = piece.astype(BF)
        for i in range(np_):
            for r, target in ((1, sends[i]), (0, keeps[i])):
                c = pltpu.make_async_copy(bufs[i].at[r, :, base:base + 16, :], target.at[:, base:base + 16, :], out_sems.at[i, 2 * blocks + r])
                c.start()
                waits.append(c)
    for c in waits:
        c.wait()


def terms(bits, parts, pairs, sums=(), factor=None):
    count = 16
    lefts, rights = zip(*pairs)
    shapes = tuple((a.shape[1], b.shape[1]) for a, b in pairs)
    tokens = lefts[0].shape[0]
    rows = sum(kin // count * (width // UNIT) for kin, width in shapes) + (16 if sums else 0)
    outs, bufs = [], []
    for cols, _ in parts:
        outs += [jax.ShapeDtypeStruct((count // 2, rows, cols), BF)] * 2
        bufs.append(pltpu.VMEM((2, count // 2, rows, cols), BF))
    flops = sum(2 * tokens * kin * width for kin, width in shapes)
    result = pl.pallas_call(
        functools.partial(terms_kernel, count, parts, shapes, bool(sums), factor is not None),
        out_shape=tuple(outs),
        in_specs=[SM] + [VM] * (factor is not None) + [HBM] * (2 * len(shapes)) + [VM] * len(sums),
        out_specs=(HBM,) * len(outs),
        scratch_shapes=[pltpu.VMEM(x.shape, BF) for x in (*lefts, *rights)]
        + bufs + [pltpu.SemaphoreType.DMA((sum(kin // 512 + width // UNIT for kin, width in shapes),)), pltpu.SemaphoreType.DMA((len(parts), 16))],
        compiler_params=pltpu.CompilerParams(vmem_limit_bytes=56 << 20),
        cost_estimate=pl.CostEstimate(flops=39000000000, bytes_accessed=113100000, transcendentals=0),
        name="terms",
    )(bits, *(() if factor is None else (factor,)), *lefts, *rights, *sums)
    return list(zip(result[::2], result[1::2]))


def swap(block, bit):
    count = lax.axis_size("dp")
    return lax.ppermute(block, "dp", [(i, i ^ (1 << bit)) for i in range(count)])


def summed(kept, came, dtype=BF):
    return (kept.astype(F32) + came.astype(F32)).astype(dtype)


def advance_kernel(bits, kept_go, came_go, kept_stay, came_stay, send, keep):
    send[...] = summed(kept_go[...], came_go[...])
    keep[...] = summed(kept_stay[...], came_stay[...])


def advance(bits, kept, came, bit):
    lead, rows, cols = kept.shape
    half = lead // 2
    block = rows
    go = pl.BlockSpec((1, block, cols), lambda g, i, b: ((1 - b[bit]) * half + g, i, 0))
    stay = pl.BlockSpec((1, block, cols), lambda g, i, b: (b[bit] * half + g, i, 0))
    out = pl.BlockSpec((1, block, cols), lambda g, i, b: (g, i, 0))
    return pl.pallas_call(
        advance_kernel,
        out_shape=(jax.ShapeDtypeStruct((half, rows, cols), BF),) * 2,
        grid_spec=pltpu.PrefetchScalarGridSpec(
            num_scalar_prefetch=1, grid=(half, rows // block), in_specs=[go, go, stay, stay], out_specs=(out, out)
        ),
        compiler_params=pltpu.CompilerParams(vmem_limit_bytes=30 << 20),
        cost_estimate=pl.CostEstimate(flops=9000000000, bytes_accessed=26100000, transcendentals=0),
        name="advance",
    )(bits, kept, came, kept, came)


def final_kernel(pieces, parts, *refs):
    n = len(parts)
    ins, outs = refs[:2 * n], refs[2 * n:]
    for (row, rows, blocks, columns), out in zip(pieces, outs):
        for q in range(blocks):
            span = slice(row + q * rows, row + (q + 1) * rows)
            if columns < UNIT:
                out[...] = summed(ins[0][0, span, 0:LANES], ins[1][0, span, 0:LANES], F32)[:, :columns]
                continue
            for i, at in enumerate(starts(parts)):
                out[:, q * UNIT + at:q * UNIT + at + parts[i][0]] = summed(ins[2 * i][0, span, :], ins[2 * i + 1][0, span, :], F32)


def final(parts, pieces, arrays):
    size = sum(a.size for a in arrays)
    return pl.pallas_call(
        functools.partial(final_kernel, pieces, parts),
        out_shape=tuple(jax.ShapeDtypeStruct((rows, blocks * columns), F32) for row, rows, blocks, columns in pieces),
        in_specs=[VM] * len(arrays),
        out_specs=(VM,) * len(pieces),
        compiler_params=pltpu.CompilerParams(vmem_limit_bytes=40 << 20),
        cost_estimate=pl.CostEstimate(flops=4500000000, bytes_accessed=13050000, transcendentals=0),
        name="final",
    )(*arrays)


def after(value, *earlier):
    return lax.optimization_barrier((value, earlier))[0]


def values_kernel(orders, offset, bits, own, *refs):
    ins, refs = refs[:6], refs[6:]
    outs, refs = refs[:4], refs[4:]
    held, mine_d, (bufs, in_sems, out_sems) = refs[:6], refs[6], refs[7:]
    width = mine_d.shape[1]
    loads = [pltpu.make_async_copy(own, mine_d, in_sems.at[0])]
    for i in (0, 1):
        kept, came, delta = ins[3 * i:3 * i + 3]
        loads += [
            pltpu.make_async_copy(kept, held[3 * i], in_sems.at[3 * i + 1]),
            pltpu.make_async_copy(came.at[:, 0:width], held[3 * i + 1], in_sems.at[3 * i + 2]),
            pltpu.make_async_copy(delta.at[:, offset:offset + width], held[3 * i + 2], in_sems.at[3 * i + 3]),
        ]
    for c in loads:
        c.start()
    loads[0].wait()
    tile = 512
    waits = []

    def dot_tn(left, right):
        return lax.dot_general(left, right, (((0,), (0,)), ((), ())), preferred_element_type=F32)

    for i in (0, 1):
        for c in loads[3 * i + 1:3 * i + 4]:
            c.wait()
        kept, came, delta = held[3 * i:3 * i + 3]

        def step(n, _, i=i, kept=kept, came=came, delta=delta):
            j, q = n // 2, n % 2
            rows = pl.ds(pl.multiple_of(j * tile, tile), tile)
            cols = pl.ds(pl.multiple_of(q * tile, tile), tile)
            res = (dot_tn(kept[:, rows], mine_d[:, cols]) + dot_tn(came[:, rows], delta[:, cols])).astype(BF)
            for s in (0, 1):
                bufs[i, j, s, :, cols] = res[s * 256:(s + 1) * 256]
            return 0

        lax.fori_loop(0, 4, step, 0)
        for j in (0, 1):
            for r, target in ((1, outs[2 * i]), (0, outs[2 * i + 1])):
                copy = pltpu.make_async_copy(bufs.at[i, j], target, out_sems.at[i, j])
                @pl.when((j ^ bits[orders[i][1]]) == r)
                def _(copy=copy):
                    copy.start()
            waits.append(copy)
    for c in waits:
        c.wait()


def values(bits, orders, offset, own, parts):
    tokens, width = own.shape
    out = jax.ShapeDtypeStruct((2, 256, width), BF)
    wide = pltpu.VMEM((tokens, width), BF)
    result = pl.pallas_call(
        functools.partial(values_kernel, orders, offset),
        out_shape=(out,) * 4,
        in_specs=[SM] + [HBM] * 7,
        out_specs=(HBM,) * 4,
        scratch_shapes=[wide] * 7 + [pltpu.VMEM((2, 2, 2, 256, width), BF), pltpu.SemaphoreType.DMA((7,)), pltpu.SemaphoreType.DMA((2, 2))],
        compiler_params=pltpu.CompilerParams(vmem_limit_bytes=56 << 20),
        cost_estimate=pl.CostEstimate(flops=30000000000, bytes_accessed=87000000, transcendentals=0),
        name="values",
    )(bits, own, *parts[0], *parts[1])
    return list(zip(result[::2], result[1::2]))


def cross_kernel(bits, kept_a, came_a, kept_b, came_b, send, keep):
    low, high = summed(kept_a[...], came_a[...]), summed(kept_b[...], came_b[...])

    @pl.when(bits[3] == 0)
    def _():
        send[...] = high
        keep[...] = low

    @pl.when(bits[3] == 1)
    def _():
        send[...] = low
        keep[...] = high


def cross(bits, arrays):
    out = jax.ShapeDtypeStruct(arrays[0].shape, BF)
    return pl.pallas_call(
        cross_kernel,
        out_shape=(out, out),
        in_specs=[SM] + [VM] * 4,
        out_specs=(VM, VM),
        compiler_params=pltpu.CompilerParams(vmem_limit_bytes=30 << 20),
        cost_estimate=pl.CostEstimate(flops=4500000000, bytes_accessed=13050000, transcendentals=0),
        name="cross",
    )(bits, *arrays)


class Line:
    def __init__(self, bits, plan, pieces):
        self.bits, self.plan, self.pieces, self.token, self.flight, self.sums = bits, plan, pieces, None, {}, {}

    def tie(self, value):
        return value if self.token is None else after(value, self.token)

    def open(self, group, pairs, sums=(), factor=None):
        pairs = ((self.tie(pairs[0][0]), pairs[0][1]),) + tuple(pairs[1:])
        found = terms(self.bits, self.plan[group], pairs, sums, factor)
        self.token = found
        for i, (send, keep) in enumerate(found):
            self.flight[group, i] = keep, swap(send, self.plan[group][i][1][0])

    def join(self, offset, own, parts):
        orders = tuple(order for _, order in self.plan["a"])
        found = values(self.bits, orders, offset, self.tie(own), parts)
        self.token = found
        for i, (send, keep) in enumerate(found):
            self.flight["a", i] = keep, swap(send, orders[i][1])

    def serve(self, steps):
        for group, i, stage in steps:
            parts = self.plan[group]
            if group == "a" and stage == 3:
                send, keep = cross(self.bits, self.tie(self.flight.pop(("a", 0)) + self.flight.pop(("a", 1))))
                self.token = send, keep
                self.flight["a", 0] = keep, swap(send, 3)
            elif group == "a" and stage == 4:
                self.sums["a"] = final(((UNIT, None),), self.pieces["a"], self.tie(list(self.flight.pop(("a", 0)))))
                self.token = self.sums["a"][0]
            elif stage < 4:
                kept, came = self.tie(self.flight[group, i])
                send, keep = advance(self.bits, kept, came, parts[i][1][stage])
                self.token = send, keep
                self.flight[group, i] = keep, swap(send, parts[i][1][stage])
            else:
                self.sums[group, i] = self.flight.pop((group, i))
                if all((group, k) in self.sums for k in range(len(parts))):
                    arrays = [a for k in range(len(parts)) for a in self.sums[group, k]]
                    arrays[0] = self.tie(arrays[0])
                    self.sums[group] = final(parts, self.pieces[group], arrays)
                    self.token = self.sums[group][0]


def halving(left, right=None):
    count = lax.axis_size("dp")
    bits = count.bit_length() - 1
    me = lax.axis_index("dp")
    if right is not None:
        left = lax.dot_general(left, right, (((0,), (0,)), ((), ())), preferred_element_type=F32).astype(BF)
    current = left.reshape((2,) * bits + (left.shape[0] // count, left.shape[1]))
    for bit in range(bits):
        axis = bits - 1 - bit
        mine = (me >> bit) & 1
        send = lax.dynamic_index_in_dim(current, 1 - mine, axis, keepdims=False)
        keep = lax.dynamic_index_in_dim(current, mine, axis, keepdims=False)
        current = summed(keep, swap(send, bit), BF if bit + 1 < bits else F32)
    return current


def unwritten(function, *args):
    shapes, tree = jax.tree.flatten(jax.eval_shape(function, *args))
    outs = pl.pallas_call(
        lambda *refs: None, out_shape=tuple(shapes), out_specs=(HBM,) * len(shapes), name="unwritten"
    )()
    return jax.tree.unflatten(tree, outs)


VECTORS = (0, 1, 5, 6, 2, 3, 4, 8, 9, 10, 11)
PARTS_0 = dict(
    a=((512, (2, 1, 0, 3)), (512, (1, 2, 0, 3))),
    b=((512, (1, 2, 0, 3)), (512, (0, 1, 2, 3))),
    e=((512, (2, 0, 1, 3)), (512, (1, 0, 2, 3))),
)
PARTS_1 = dict(
    a=((512, (1, 2, 0, 3)), (512, (2, 1, 0, 3))),
    b=((512, (2, 0, 1, 3)), (512, (0, 2, 1, 3))),
    e=((512, (1, 0, 2, 3)), (512, (2, 0, 1, 3))),
)
ORDER_1 = ('a', 'b', 'e')
STEPS_0 = (('a', 1, 2), ('b', 0, 1), ('a', 0, 2), ('b', 1, 1), ('e', 1, 1), ('e', 0, 1), ('a', 0, 3), ('b', 1, 2), ('b', 0, 2), ('e', 1, 2), ('a', 0, 4), ('e', 0, 2), ('b', 1, 3), ('b', 0, 3), ('e', 0, 3), ('e', 1, 3), ('b', 1, 4), ('b', 0, 4), ('e', 0, 4), ('e', 1, 4))
STEPS_1 = (('a', 0, 2), ('a', 1, 2), ('b', 0, 1), ('e', 0, 1), ('b', 1, 1), ('e', 1, 1), ('a', 0, 3), ('b', 1, 2), ('b', 0, 2), ('a', 0, 4), ('b', 1, 3), ('b', 0, 3), ('e', 0, 2), ('b', 1, 4), ('b', 0, 4), ('e', 1, 2), ('e', 0, 3), ('e', 1, 3), ('e', 0, 4), ('e', 1, 4))


def local(entry_pair, labels, *params):
    count = lax.axis_size("dp")
    section = lax.axis_index("section")
    rows, each, width = entry_pair.shape[1:]
    own = entry_pair.reshape(rows * each, width)
    share = width // count
    p = [e if e.ndim == 2 else e[0] for e in params]
    ff = p[15].shape[1]
    first = jnp.zeros((rows, 1), F32)
    same_s = jnp.concatenate([first, (labels[:, 1:] == labels[:, :-1]).astype(F32)], axis=1)
    same = jnp.broadcast_to(same_s.reshape(rows * each, 1), (rows * each, LANES))
    fast = count == 16 and width == UNIT
    me = lax.axis_index("dp")
    bits = jnp.stack([(me >> i) & 1 for i in range(4)])
    wide = ff // width
    pieces = dict(
        a=((0, ff // count, 1, width),),
        b=((0, share, wide, width), (share * wide, share, 1, width), (share * (wide + 1), share, 1, width)),
        e=tuple((i * share, share, 1, width) for i in range(3)) + tuple((3 * share + i, 1, 1, share) for i in VECTORS),
    )

    def plain_rest(pairs, sums):
        together = jnp.concatenate(sums).astype(BF).reshape(16, count, share).transpose(1, 0, 2).reshape(count * 16, share)
        vectors = halving(together)
        return tuple(halving(*pair) for pair in pairs) + tuple(vectors[i:i + 1] for i in VECTORS)

    def orders(plan):
        return tuple(order for _, order in plan["a"]) if fast else None

    def start():
        return forward(rows, False, same_s, same, own, p, own, bits, orders(PARTS_0))

    def middle_part(received):
        kept = forward(rows, True, same_s, same, received, p, own, bits, orders(PARTS_1))
        (key_in, value_in, recept_in, ks, vs, gate, tops, bottoms, mixed, middle, hidden_in, gate_in, act, result, delta_out, delta_gate, mean, scale, mean2, scale2, *acts) = kept
        begun = act, delta_out
        if fast:
            came = [swap(acts[2 * i], PARTS_1["a"][i][1][0]) for i in (0, 1)]
            begun = delta_out, [(acts[2 * i + 1], came[i]) for i in (0, 1)]
        g = after(own, acts[0]) if fast else own
        delta_pre, delta, branch, late, _, _ = channel(rows, False, same, delta_out, delta_gate, g, p, act, middle, mean2, scale2)
        dk, dv, dr, state, early = time_mix(rows, BF, same_s, same, branch, delta, received, p, gate, ks, vs, tops, bottoms, mean, scale)
        key_pairs = ((hidden_in, delta_pre), (gate_in, delta_gate), (mixed, branch))
        return state, result, begun, (early, late), key_pairs, ((key_in, dk), (value_in, dv), (recept_in, dr))

    def end_first(received, kept, acts_came):
        (key_in, value_in, recept_in, ks, vs, gate, tops, bottoms, mixed, middle, hidden_in, gate_in, act, result, factor_out, factor_gate, mean, scale, mean2, scale2, *acts) = kept
        line = Line(bits, PARTS_0, pieces)
        if fast:
            own_delta = (received.astype(F32) * factor_out.astype(F32)).astype(BF)
            came = [swap(own_delta, PARTS_0["a"][i][1][0]) for i in (0, 1)]
            line.token = own_delta
        g = line.tie(received)
        delta_pre, delta, branch, late, delta_out, delta_gate = channel(rows, True, same, factor_out, factor_gate, g, p, act, middle, mean2, scale2)
        key_pairs = ((hidden_in, delta_pre), (gate_in, delta_gate), (mixed, branch))
        line.token = branch
        if fast:
            line.open("b", key_pairs)
            line.join(0, own_delta, [(acts[2 * i + 1], acts_came[i], came[i]) for i in (0, 1)])
        dk, dv, dr, state, early = time_mix(rows, F32, same_s, same, line.tie(branch), delta, own, p, gate, ks, vs, tops, bottoms, mean, scale)
        rest_pairs = ((key_in, dk), (value_in, dv), (recept_in, dr))
        if not fast:
            return state, (halving(act, delta_out),), tuple(halving(*pair) for pair in key_pairs), plain_rest(rest_pairs, (early, late))
        line.token = state
        line.open("e", rest_pairs, (early, late))
        line.serve(STEPS_0)
        return state, line.sums["a"], line.sums["b"], line.sums["e"]

    def end_second(result, begun, sums, key_pairs, rest_pairs):
        if not fast:
            return result.astype(F32), (halving(*begun),), tuple(halving(*pair) for pair in key_pairs), plain_rest(rest_pairs, sums)
        line = Line(bits, PARTS_1, pieces)
        for name in ORDER_1:
            if name == "a":
                line.join(width, begun[0], [(kept, came, came) for kept, came in begun[1]])
            elif name == "b":
                line.open("b", key_pairs)
            else:
                line.open("e", rest_pairs, sums)
        line.serve(STEPS_1)
        return result.astype(F32), line.sums["a"], line.sums["b"], line.sums["e"]

    def swap_first(block, bit):
        return lax.ppermute(block, ("section", "dp"), [(i, i ^ (1 << bit)) for i in range(count)])

    kept = lax.cond(section == 0, start, lambda: unwritten(start))
    received = lax.ppermute(kept[13], "section", [(0, 1)])
    acts_came = [swap_first(kept[20 + 2 * i], PARTS_0["a"][i][1][0]) for i in (0, 1)] if fast else []
    delta, *pending = lax.cond(section == 1, middle_part, lambda r: unwritten(middle_part, r), received)
    received = lax.ppermute(delta, "section", [(1, 0)])
    ends, (value_sum,), (key_sum, gate_sum, exit_sum), rest = lax.cond(
        section == 0, lambda r, k, a, q: end_first(r, k, a), lambda r, k, a, q: end_second(*q), received, kept, acts_came, pending
    )
    ends = ends.reshape(rows, each, width)
    everything = (ends, *(z[0] for z in rest[3:10]), *rest[:3], exit_sum, *(z[0] for z in rest[10:14]), key_sum, gate_sum, value_sum)
    return tuple(e[None] for e in everything)


def solution(mesh):
    vec, mat = P("section", None), P("section", None, None)
    in_specs = (P("section", "dp", None, None), P("dp", None)) + (vec,) * 7 + (mat,) * 4 + (vec,) * 4 + (mat,) * 3
    vec, mat = P("section", "dp"), P("section", "dp", None)
    out_specs = (P("section", "dp", None, None),) + (vec,) * 7 + (mat,) * 4 + (vec,) * 4 + (mat,) * 3
    return jax.shard_map(local, mesh=mesh, in_specs=in_specs, out_specs=out_specs, check_vma=False)
```

profile of v0, /device:TPU:0, one launch (start us, length us, event | category | flops | bytes accessed | tf_op | source)
XLA Modules:
  0.0 333.6 jit_solution(6165314361148672866)
XLA Ops:
  1.8 28.8 %conditional.3 = ((bf16[512,1024]{1,0:T(8,128)(2,1)}, bf16[512,1024]{1,0:T(8,128)(2,1)}, bf16[512,1024]{1,0:T(8,128)(2,1)}, f32[4096,128]{1,0:T(8,128)}, f32[409...) conditional(s32[]{:T(128)} %convert_element_type.18, () %tuple.78, ...), branch_computations={%region_0.0_spmd, %region_1.0_spmd} | conditional | flops 89999998976 | bytes 261000000 | solution.py:959
  1.8 28.8 %forward.2 = (bf16[512,1024]{1,0:T(8,128)(2,1)}, bf16[512,1024]{1,0:T(8,128)(2,1)}, bf16[512,1024]{1,0:T(8,128)(2,1)}, f32[4096,128]{1,0:T(8,128)}, f32[4096,128...) custom-call(s32[4]{0:T(128)S(1)} %get-tuple-element.226.refs_0_, ...), custom_call_target="tpu_custom_call" | custom-call | flops 89999998976 | bytes 261000000 | tf_op jit(solution)/shard_map/cond/branch_1_fun/forward/pallas_call | solution.py:239
  31.9 5.0 %collective-permute-start.48 = (bf16[512,1024]{1,0:T(8,128)(2,1)}, bf16[512,1024]{1,0:T(8,128)(2,1)}, u32[]{:S(2)}, u32[]{:S(2)}) collective-permute-start(bf16[512,1024]{1,0:T(8,128)(2,1)} %get-tuple-element.694), channel_id=1, source_target_pairs={{0,4},{1,5},{2,6},{3,7},{4,0},{5,1},{6,2},{7,3},{8,12},{9,13},{10,... | collective-permute-start | bytes 3145736 | tf_op jit(solution)/shard_map/ppermute | solution.py:957
  36.9 3.4 %collective-permute-start.49 = (bf16[512,1024]{1,0:T(8,128)(2,1)}, bf16[512,1024]{1,0:T(8,128)(2,1)}, u32[]{:S(2)}, u32[]{:S(2)}) collective-permute-start(bf16[512,1024]{1,0:T(8,128)(2,1)} %get-tuple-element.696), channel_id=1, source_target_pairs={{0,2},{1,3},{2,0},{3,1},{4,6},{5,7},{6,4},{7,5},{8,10},{9,11},{10,... | collective-permute-start | bytes 3145736 | tf_op jit(solution)/shard_map/ppermute | solution.py:957
  40.3 9.2 %conditional.4 = ((bf16[512,1024]{1,0:T(8,128)(2,1)}, bf16[512,1024]{1,0:T(8,128)(2,1)}, bf16[512,1024]{1,0:T(8,128)(2,1)}, bf16[512,1024]{1,0:T(8,128)(2,1)}, b...) conditional(s32[]{:T(128)} %convert_element_type.19, () %tuple.77, ...), branch_computations={%region_2.0_spmd, %region_3.0_spmd} | conditional | flops 251999977472 | bytes 764445248 | solution.py:962
  53.9 62.7 %collective-permute-done.47 = bf16[512,1024]{1,0:T(8,128)(2,1)} collective-permute-done((bf16[512,1024]{1,0:T(8,128)(2,1)}, bf16[512,1024]{1,0:T(8,128)(2,1)}, u32[]{:S(2)}, u32[]{:S(2)}) %collective-permute-start.47) | collective-permute-done | bytes 1048608 | tf_op jit(solution)/shard_map/ppermute | solution.py:963
  116.6 215.7 %conditional.5 = (f32[64,4096]{1,0:T(8,128)}, f32[64,1024]{1,0:T(8,128)}, f32[64,1024]{1,0:T(8,128)}, f32[64,1024]{1,0:T(8,128)}, f32[64,1024]{1,0:T(8,128)}, /*...) conditional(s32[]{:T(128)} %convert_element_type.18, ...), branch_computations={%region_4.0_spmd, %region_5.0_spmd} | conditional | flops 414001987584 | bytes 1378309504 | solution.py:964
  120.4 21.8 %channel.3 = (bf16[512,4096]{1,0:T(8,128)(2,1)}, f32[512,1024]{1,0:T(8,128)}, bf16[512,1024]{1,0:T(8,128)(2,1)}, f32[8,1024]{1,0:T(8,128)}, bf16[512,1024]{1,0:T(8,128)(2,1)}, /*index=5*/bf16[512,1024]{1,0:T(8,128)(2,1)}) custom-call(f32[512,128]{1,0:T(8,128)S(1)} %copy-done.16, bf16[512,1024]{1,0:T(8,128)(2,1)S(1)} %copy-done.13, ...), custom_call_target="tpu_custom_call" | custom-call | flops 74999996416 | bytes 217500000 | tf_op jit(solution)/shard_map/cond/branch_1_fun/channel/pallas_call | solution.py:374
  142.2 12.7 %terms.6 = (bf16[8,384,512]{2,1,0:T(8,128)(2,1)}, bf16[8,384,512]{2,1,0:T(8,128)(2,1)}, bf16[8,384,512]{2,1,0:T(8,128)(2,1)}, bf16[8,384,512]{2,1,0:T(8,128)(2,1)}) custom-call(s32[4]{0:T(128)S(1)} %copy-done.22, bf16[512,1024]{1,0:T(8,128)(2,1)} %get-tuple-element.442.refs_1_, bf16[512,1024]{1,0:T(8,128)(2,1)} %get-tuple-element.443.refs_2_, ...), custom_call_target="tpu_custom_call" | custom-call | flops 38999998464 | bytes 113100000 | tf_op jit(solution)/shard_map/cond/branch_1_fun/terms/pallas_call | solution.py:620
  159.2 9.8 %values.3 = (bf16[2,256,1024]{2,1,0:T(8,128)(2,1)}, bf16[2,256,1024]{2,1,0:T(8,128)(2,1)}, bf16[2,256,1024]{2,1,0:T(8,128)(2,1)}, bf16[2,256,1024]{2,1,0:T(8,128)(2,1)}) custom-call(s32[4]{0:T(128)S(1)} %copy-done.22, bf16[512,1024]{1,0:T(8,128)(2,1)} %copy-done.12, bf16[512,1024]{1,0:T(8,128)(2,1)S(1)} %copy-done.52, ...), custom_call_target="tpu_custom_call" | custom-call | flops 30000001024 | bytes 87000000 | tf_op jit(solution)/shard_map/cond/branch_1_fun/values/pallas_call | solution.py:749
  171.2 21.3 %time_mix.3 = (bf16[512,1024]{1,0:T(8,128)(2,1)}, bf16[512,1024]{1,0:T(8,128)(2,1)}, bf16[512,1024]{1,0:T(8,128)(2,1)}, f32[512,1024]{1,0:T(8,128)}, f32[8,1024]{1,0:T(8,128)}) custom-call(f32[2,256]{1,0:T(2,128)S(1)} %copy-done.18, f32[512,128]{1,0:T(8,128)S(1)} %copy-done.16, bf16[512,1024]{1,0:T(8,128)(2,1)} %get-tuple-element.462.refs_6_.refs_2_, ...), custom_call_target="tpu_custom_call" | custom-call | flops 86999998464 | bytes 252300000 | tf_op jit(solution)/shard_map/cond/branch_1_fun/time_mix/pallas_call | solution.py:491
  192.5 8.6 %terms.7 = (bf16[8,208,512]{2,1,0:T(8,128)(2,1)}, bf16[8,208,512]{2,1,0:T(8,128)(2,1)}, bf16[8,208,512]{2,1,0:T(8,128)(2,1)}, bf16[8,208,512]{2,1,0:T(8,128)(2,1)}) custom-call(s32[4]{0:T(128)S(1)} %copy-done.22, bf16[512,1024]{1,0:T(8,128)(2,1)} %get-tuple-element.484.refs_1_, bf16[512,1024]{1,0:T(8,128)(2,1)} %get-tuple-element.485.refs_2_, ...), custom_call_target="tpu_custom_call" | custom-call | flops 38999998464 | bytes 113100000 | tf_op jit(solution)/shard_map/cond/branch_1_fun/terms/pallas_call | solution.py:620
  206.8 3.6 %advance.43 = (bf16[4,384,512]{2,1,0:T(8,128)(2,1)S(1)}, bf16[4,384,512]{2,1,0:T(8,128)(2,1)S(1)}) custom-call(s32[4]{0:T(128)S(1)} %copy-done.22, bf16[8,384,512]{2,1,0:T(8,128)(2,1)S(1)} %copy-done.1, bf16[8,384,512]{2,1,0:T(8,128)(2,1)} %collective-permute-done.23.came_go.came_stay, bf16[8,384,512]{2,1,0:T(8,128)(2,1)S(1)} %copy-done.1, ...), custom_call_target="tpu_custom_call" | custom-call | flops 8999999488 | bytes 26100000 | tf_op jit(solution)/shard_map/cond/branch_1_fun/advance/pallas_call | solution.py:655
  210.4 6.9 %collective-permute-done.29.came_go.came_stay = bf16[2,256,1024]{2,1,0:T(8,128)(2,1)S(1)} collective-permute-done((bf16[2,256,1024]{2,1,0:T(8,128)(2,1)}, bf16[2,256,1024]{2,1,0:T(8,128)(2,1)S(1)}, u32[]{:S(2)}, u32[]{:S(2)}) %collective-permute-start.29) | collective-permute-done | bytes 1048608 | tf_op jit(solution)/shard_map/cond/branch_1_fun/ppermute | solution.py:636
  218.6 5.0 %collective-permute-done.28.came_go.came_stay = bf16[8,384,512]{2,1,0:T(8,128)(2,1)} collective-permute-done((bf16[8,384,512]{2,1,0:T(8,128)(2,1)}, bf16[8,384,512]{2,1,0:T(8,128)(2,1)}, u32[]{:S(2)}, u32[]{:S(2)}) %collective-permute-start.28) | collective-permute-done | bytes 3145760 | tf_op jit(solution)/shard_map/cond/branch_1_fun/ppermute | solution.py:636
  225.1 3.6 %advance.45 = (bf16[4,384,512]{2,1,0:T(8,128)(2,1)S(1)}, bf16[4,384,512]{2,1,0:T(8,128)(2,1)S(1)}) custom-call(s32[4]{0:T(128)S(1)} %copy-done.22, bf16[8,384,512]{2,1,0:T(8,128)(2,1)S(1)} %copy-done, bf16[8,384,512]{2,1,0:T(8,128)(2,1)} %collective-permute-done.28.came_go.came_stay, bf16[8,384,512]{2,1,0:T(8,128)(2,1)S(1)} %copy-done, ...), custom_call_target="tpu_custom_call" | custom-call | flops 8999999488 | bytes 26100000 | tf_op jit(solution)/shard_map/cond/branch_1_fun/advance/pallas_call | solution.py:655
  228.7 6.9 %collective-permute-done.34.came_go.came_stay = bf16[8,208,512]{2,1,0:T(8,128)(2,1)S(1)} collective-permute-done((bf16[8,208,512]{2,1,0:T(8,128)(2,1)}, bf16[8,208,512]{2,1,0:T(8,128)(2,1)S(1)}, u32[]{:S(2)}, u32[]{:S(2)}) %collective-permute-start.34) | collective-permute-done | bytes 1703968 | tf_op jit(solution)/shard_map/cond/branch_1_fun/ppermute | solution.py:636
  238.2 9.0 %collective-permute-done.33.came_go.came_stay = bf16[8,208,512]{2,1,0:T(8,128)(2,1)S(1)} collective-permute-done((bf16[8,208,512]{2,1,0:T(8,128)(2,1)}, bf16[8,208,512]{2,1,0:T(8,128)(2,1)S(1)}, u32[]{:S(2)}, u32[]{:S(2)}) %collective-permute-start.33) | collective-permute-done | bytes 1703968 | tf_op jit(solution)/shard_map/cond/branch_1_fun/ppermute | solution.py:636
  252.0 4.0 %collective-permute-done.30.came_go.came_stay = bf16[4,384,512]{2,1,0:T(8,128)(2,1)S(1)} collective-permute-done((bf16[4,384,512]{2,1,0:T(8,128)(2,1)S(1)}, bf16[4,384,512]{2,1,0:T(8,128)(2,1)S(1)}, u32[]{:S(2)}, u32[]{:S(2)}) %collective-permute-start.30) | collective-permute-done | bytes 1572896 | tf_op jit(solution)/shard_map/cond/branch_1_fun/ppermute | solution.py:636
  258.1 14.3 %collective-permute-done.27.came_go.came_stay = bf16[4,384,512]{2,1,0:T(8,128)(2,1)S(1)} collective-permute-done((bf16[4,384,512]{2,1,0:T(8,128)(2,1)S(1)}, bf16[4,384,512]{2,1,0:T(8,128)(2,1)S(1)}, u32[]{:S(2)}, u32[]{:S(2)}) %collective-permute-start.27) | collective-permute-done | bytes 1572896 | tf_op jit(solution)/shard_map/cond/branch_1_fun/ppermute | solution.py:636
  275.9 11.4 %collective-permute-done.37.came_go.came_stay = bf16[4,208,512]{2,1,0:T(8,128)(2,1)S(1)} collective-permute-done((bf16[4,208,512]{2,1,0:T(8,128)(2,1)S(1)}, bf16[4,208,512]{2,1,0:T(8,128)(2,1)S(1)}, u32[]{:S(2)}, u32[]{:S(2)}) %collective-permute-start.37) | collective-permute-done | bytes 852000 | tf_op jit(solution)/shard_map/cond/branch_1_fun/ppermute | solution.py:636
  291.1 5.0 %collective-permute-done.35.came_go.came_stay = bf16[2,384,512]{2,1,0:T(8,128)(2,1)S(1)} collective-permute-done((bf16[2,384,512]{2,1,0:T(8,128)(2,1)S(1)}, bf16[2,384,512]{2,1,0:T(8,128)(2,1)S(1)}, u32[]{:S(2)}, u32[]{:S(2)}) %collective-permute-start.35) | collective-permute-done | bytes 786464 | tf_op jit(solution)/shard_map/cond/branch_1_fun/ppermute | solution.py:636
  303.8 22.2 %collective-permute-done.42.refs_1_ = bf16[1,384,512]{2,1,0:T(8,128)(2,1)S(1)} collective-permute-done((bf16[1,384,512]{2,1,0:T(8,128)(2,1)S(1)}, bf16[1,384,512]{2,1,0:T(8,128)(2,1)S(1)}, u32[]{:S(2)}, u32[]{:S(2)}) %collective-permute-start.42) | collective-permute-done | bytes 393248 | tf_op jit(solution)/shard_map/cond/branch_1_fun/ppermute | solution.py:636
  327.2 3.9 %collective-permute-done.45.refs_3_ = bf16[1,208,512]{2,1,0:T(8,128)(2,1)S(1)} collective-permute-done((bf16[1,208,512]{2,1,0:T(8,128)(2,1)S(1)}, bf16[1,208,512]{2,1,0:T(8,128)(2,1)S(1)}, u32[]{:S(2)}, u32[]{:S(2)}) %collective-permute-start.45) | collective-permute-done | bytes 213024 | tf_op jit(solution)/shard_map/cond/branch_1_fun/ppermute | solution.py:636
  (132 shorter events, 52.8 us)
Async XLA Ops:
  31.9 18.9 %collective-permute-start.48 = (bf16[512,1024]{1,0:T(8,128)(2,1)}, bf16[512,1024]{1,0:T(8,128)(2,1)}, u32[]{:S(2)}, u32[]{:S(2)}) collective-permute-start(bf16[512,1024]{1,0:T(8,128)(2,1)} %get-tuple-element.694), channel_id=1, source_target_pairs={{0,4},{1,5},{2,6},{3,7},{4,0},{5,1},{6,2},{7,3},{8,12},{9,13},{10,... | collective-permute-start | bytes 3145736 | tf_op jit(solution)/shard_map/ppermute | solution.py:957
  49.5 67.1 %collective-permute-start.47 = (bf16[512,1024]{1,0:T(8,128)(2,1)}, bf16[512,1024]{1,0:T(8,128)(2,1)}, u32[]{:S(2)}, u32[]{:S(2)}) collective-permute-start(bf16[512,1024]{1,0:T(8,128)(2,1)} %get-tuple-element.683), channel_id=1, source_target_pairs={{16,0},{17,1},{18,2},{19,3},{20,4},{21,5},{22,6},{23,7},{24,8},{25... | collective-permute-start | bytes 3145736 | tf_op jit(solution)/shard_map/ppermute | solution.py:963
  119.3 38.8 %collective-permute-start.25 = (bf16[512,1024]{1,0:T(8,128)(2,1)S(1)}, bf16[512,1024]{1,0:T(8,128)(2,1)S(1)}, u32[]{:S(2)}, u32[]{:S(2)}) collective-permute-start(bf16[512,1024]{1,0:T(8,128)(2,1)S(1)} %multiply_convert_fusion.own), channel_id=1, source_target_pairs={{0,2},{1,3},{2,0},{3,1},{4,6},{5,7},{6,4},{7,5},{8,10},{9,11},{10,... | collective-permute-start | bytes 3145736 | tf_op jit(solution)/shard_map/cond/branch_1_fun/ppermute | solution.py:636
  119.9 38.2 %collective-permute-start.24 = (bf16[512,1024]{1,0:T(8,128)(2,1)S(1)}, bf16[512,1024]{1,0:T(8,128)(2,1)}, u32[]{:S(2)}, u32[]{:S(2)}) collective-permute-start(bf16[512,1024]{1,0:T(8,128)(2,1)S(1)} %multiply_convert_fusion.own), channel_id=1, source_target_pairs={{0,4},{1,5},{2,6},{3,7},{4,0},{5,1},{6,2},{7,3},{8,12},{9,13},{10,... | collective-permute-start | bytes 3145736 | tf_op jit(solution)/shard_map/cond/branch_1_fun/ppermute | solution.py:636
  154.9 51.3 %collective-permute-start.23 = (bf16[8,384,512]{2,1,0:T(8,128)(2,1)}, bf16[8,384,512]{2,1,0:T(8,128)(2,1)}, u32[]{:S(2)}, u32[]{:S(2)}) collective-permute-start(bf16[8,384,512]{2,1,0:T(8,128)(2,1)} %get-tuple-element.448), channel_id=1, source_target_pairs={{0,2},{1,3},{2,0},{3,1},{4,6},{5,7},{6,4},{7,5},{8,10},{9,11},{10,... | collective-permute-start | bytes 9437192 | tf_op jit(solution)/shard_map/cond/branch_1_fun/ppermute | solution.py:636
  156.6 67.0 %collective-permute-start.28 = (bf16[8,384,512]{2,1,0:T(8,128)(2,1)}, bf16[8,384,512]{2,1,0:T(8,128)(2,1)}, u32[]{:S(2)}, u32[]{:S(2)}) collective-permute-start(bf16[8,384,512]{2,1,0:T(8,128)(2,1)} %get-tuple-element.449), channel_id=1, source_target_pairs={{0,1},{1,0},{2,3},{3,2},{4,5},{5,4},{6,7},{7,6},{8,9},{9,8},{10,11... | collective-permute-start | bytes 9437192 | tf_op jit(solution)/shard_map/cond/branch_1_fun/ppermute | solution.py:636
  169.0 32.6 %collective-permute-start.26 = (bf16[2,256,1024]{2,1,0:T(8,128)(2,1)}, bf16[2,256,1024]{2,1,0:T(8,128)(2,1)S(1)}, u32[]{:S(2)}, u32[]{:S(2)}) collective-permute-start(bf16[2,256,1024]{2,1,0:T(8,128)(2,1)} %get-tuple-element.457), channel_id=1, source_target_pairs={{0,4},{1,5},{2,6},{3,7},{4,0},{5,1},{6,2},{7,3},{8,12},{9,13},{10,... | collective-permute-start | bytes 3145736 | tf_op jit(solution)/shard_map/cond/branch_1_fun/ppermute | solution.py:636
  170.6 46.7 %collective-permute-start.29 = (bf16[2,256,1024]{2,1,0:T(8,128)(2,1)}, bf16[2,256,1024]{2,1,0:T(8,128)(2,1)S(1)}, u32[]{:S(2)}, u32[]{:S(2)}) collective-permute-start(bf16[2,256,1024]{2,1,0:T(8,128)(2,1)} %get-tuple-element.460), channel_id=1, source_target_pairs={{0,2},{1,3},{2,0},{3,1},{4,6},{5,7},{6,4},{7,5},{8,10},{9,11},{10,... | collective-permute-start | bytes 3145736 | tf_op jit(solution)/shard_map/cond/branch_1_fun/ppermute | solution.py:636
  201.1 46.0 %collective-permute-start.33 = (bf16[8,208,512]{2,1,0:T(8,128)(2,1)}, bf16[8,208,512]{2,1,0:T(8,128)(2,1)S(1)}, u32[]{:S(2)}, u32[]{:S(2)}) collective-permute-start(bf16[8,208,512]{2,1,0:T(8,128)(2,1)} %get-tuple-element.492), channel_id=1, source_target_pairs={{0,4},{1,5},{2,6},{3,7},{4,0},{5,1},{6,2},{7,3},{8,12},{9,13},{10,... | collective-permute-start | bytes 5111816 | tf_op jit(solution)/shard_map/cond/branch_1_fun/ppermute | solution.py:636
  201.6 34.0 %collective-permute-start.34 = (bf16[8,208,512]{2,1,0:T(8,128)(2,1)}, bf16[8,208,512]{2,1,0:T(8,128)(2,1)S(1)}, u32[]{:S(2)}, u32[]{:S(2)}) collective-permute-start(bf16[8,208,512]{2,1,0:T(8,128)(2,1)} %get-tuple-element.494), channel_id=1, source_target_pairs={{0,2},{1,3},{2,0},{3,1},{4,6},{5,7},{6,4},{7,5},{8,10},{9,11},{10,... | collective-permute-start | bytes 5111816 | tf_op jit(solution)/shard_map/cond/branch_1_fun/ppermute | solution.py:636
  206.2 42.5 %collective-permute-start.32 = (bf16[1,256,1024]{2,1,0:T(8,128)(2,1)S(1)}, bf16[1,256,1024]{2,1,0:T(8,128)(2,1)S(1)}, u32[]{:S(2)}, u32[]{:S(2)}) collective-permute-start(bf16[1,256,1024]{2,1,0:T(8,128)(2,1)S(1)} %get-tuple-element.498), channel_id=1, source_target_pairs={{0,1},{1,0},{2,3},{3,2},{4,5},{5,4},{6,7},{7,6},{8,9},{9,8},{10,11... | collective-permute-start | bytes 1572872 | tf_op jit(solution)/shard_map/cond/branch_1_fun/ppermute | solution.py:636
  217.4 55.0 %collective-permute-start.27 = (bf16[4,384,512]{2,1,0:T(8,128)(2,1)S(1)}, bf16[4,384,512]{2,1,0:T(8,128)(2,1)S(1)}, u32[]{:S(2)}, u32[]{:S(2)}) collective-permute-start(bf16[4,384,512]{2,1,0:T(8,128)(2,1)S(1)} %get-tuple-element.503), channel_id=1, source_target_pairs={{0,4},{1,5},{2,6},{3,7},{4,0},{5,1},{6,2},{7,3},{8,12},{9,13},{10,... | collective-permute-start | bytes 4718600 | tf_op jit(solution)/shard_map/cond/branch_1_fun/ppermute | solution.py:636
  223.6 26.7 %collective-permute-start.31 = (bf16[1,256,1024]{2,1,0:T(8,128)(2,1)S(1)}, bf16[1,256,1024]{2,1,0:T(8,128)(2,1)S(1)}, u32[]{:S(2)}, u32[]{:S(2)}) collective-permute-start(bf16[1,256,1024]{2,1,0:T(8,128)(2,1)S(1)} %get-tuple-element.506), channel_id=1, source_target_pairs={{0,1},{1,0},{2,3},{3,2},{4,5},{5,4},{6,7},{7,6},{8,9},{9,8},{10,11... | collective-permute-start | bytes 1572872 | tf_op jit(solution)/shard_map/cond/branch_1_fun/ppermute | solution.py:636
  235.6 20.4 %collective-permute-start.30 = (bf16[4,384,512]{2,1,0:T(8,128)(2,1)S(1)}, bf16[4,384,512]{2,1,0:T(8,128)(2,1)S(1)}, u32[]{:S(2)}, u32[]{:S(2)}) collective-permute-start(bf16[4,384,512]{2,1,0:T(8,128)(2,1)S(1)} %get-tuple-element.511), channel_id=1, source_target_pairs={{0,2},{1,3},{2,0},{3,1},{4,6},{5,7},{6,4},{7,5},{8,10},{9,11},{10,... | collective-permute-start | bytes 4718600 | tf_op jit(solution)/shard_map/cond/branch_1_fun/ppermute | solution.py:636
  247.1 27.7 %collective-permute-start.39 = (bf16[4,208,512]{2,1,0:T(8,128)(2,1)S(1)}, bf16[4,208,512]{2,1,0:T(8,128)(2,1)S(1)}, u32[]{:S(2)}, u32[]{:S(2)}) collective-permute-start(bf16[4,208,512]{2,1,0:T(8,128)(2,1)S(1)} %get-tuple-element.514), channel_id=1, source_target_pairs={{0,1},{1,0},{2,3},{3,2},{4,5},{5,4},{6,7},{7,6},{8,9},{9,8},{10,11... | collective-permute-start | bytes 2555912 | tf_op jit(solution)/shard_map/cond/branch_1_fun/ppermute | solution.py:636
  248.7 38.5 %collective-permute-start.37 = (bf16[4,208,512]{2,1,0:T(8,128)(2,1)S(1)}, bf16[4,208,512]{2,1,0:T(8,128)(2,1)S(1)}, u32[]{:S(2)}, u32[]{:S(2)}) collective-permute-start(bf16[4,208,512]{2,1,0:T(8,128)(2,1)S(1)} %get-tuple-element.518), channel_id=1, source_target_pairs={{0,1},{1,0},{2,3},{3,2},{4,5},{5,4},{6,7},{7,6},{8,9},{9,8},{10,11... | collective-permute-start | bytes 2555912 | tf_op jit(solution)/shard_map/cond/branch_1_fun/ppermute | solution.py:636
  251.3 24.4 %collective-permute-start.38 = (bf16[1,256,1024]{2,1,0:T(8,128)(2,1)S(1)}, bf16[1,256,1024]{2,1,0:T(8,128)(2,1)S(1)}, u32[]{:S(2)}, u32[]{:S(2)}) collective-permute-start(bf16[1,256,1024]{2,1,0:T(8,128)(2,1)S(1)} %get-tuple-element.524), channel_id=1, source_target_pairs={{0,8},{1,9},{2,10},{3,11},{4,12},{5,13},{6,14},{7,15},{8,0},{9,1},... | collective-permute-start | bytes 1572872 | tf_op jit(solution)/shard_map/cond/branch_1_fun/ppermute | solution.py:636
  257.0 32.7 %collective-permute-start.36 = (bf16[2,384,512]{2,1,0:T(8,128)(2,1)S(1)}, bf16[2,384,512]{2,1,0:T(8,128)(2,1)S(1)}, u32[]{:S(2)}, u32[]{:S(2)}) collective-permute-start(bf16[2,384,512]{2,1,0:T(8,128)(2,1)S(1)} %get-tuple-element.528), channel_id=1, source_target_pairs={{0,4},{1,5},{2,6},{3,7},{4,0},{5,1},{6,2},{7,3},{8,12},{9,13},{10,... | collective-permute-start | bytes 2359304 | tf_op jit(solution)/shard_map/cond/branch_1_fun/ppermute | solution.py:636
  273.3 22.8 %collective-permute-start.35 = (bf16[2,384,512]{2,1,0:T(8,128)(2,1)S(1)}, bf16[2,384,512]{2,1,0:T(8,128)(2,1)S(1)}, u32[]{:S(2)}, u32[]{:S(2)}) collective-permute-start(bf16[2,384,512]{2,1,0:T(8,128)(2,1)S(1)} %get-tuple-element.533), channel_id=1, source_target_pairs={{0,1},{1,0},{2,3},{3,2},{4,5},{5,4},{6,7},{7,6},{8,9},{9,8},{10,11... | collective-permute-start | bytes 2359304 | tf_op jit(solution)/shard_map/cond/branch_1_fun/ppermute | solution.py:636
  275.7 24.9 %collective-permute-start.40 = (bf16[2,208,512]{2,1,0:T(8,128)(2,1)S(1)}, bf16[2,208,512]{2,1,0:T(8,128)(2,1)S(1)}, u32[]{:S(2)}, u32[]{:S(2)}) collective-permute-start(bf16[2,208,512]{2,1,0:T(8,128)(2,1)S(1)} %get-tuple-element.536), channel_id=1, source_target_pairs={{0,4},{1,5},{2,6},{3,7},{4,0},{5,1},{6,2},{7,3},{8,12},{9,13},{10,... | collective-permute-start | bytes 1277960 | tf_op jit(solution)/shard_map/cond/branch_1_fun/ppermute | solution.py:636
  290.4 35.6 %collective-permute-start.43 = (bf16[1,384,512]{2,1,0:T(8,128)(2,1)S(1)}, bf16[1,384,512]{2,1,0:T(8,128)(2,1)S(1)}, u32[]{:S(2)}, u32[]{:S(2)}) collective-permute-start(bf16[1,384,512]{2,1,0:T(8,128)(2,1)S(1)} %get-tuple-element.546), channel_id=1, source_target_pairs={{0,8},{1,9},{2,10},{3,11},{4,12},{5,13},{6,14},{7,15},{8,0},{9,1},... | collective-permute-start | bytes 1179656 | tf_op jit(solution)/shard_map/cond/branch_1_fun/ppermute | solution.py:636
  296.8 29.2 %collective-permute-start.42 = (bf16[1,384,512]{2,1,0:T(8,128)(2,1)S(1)}, bf16[1,384,512]{2,1,0:T(8,128)(2,1)S(1)}, u32[]{:S(2)}, u32[]{:S(2)}) collective-permute-start(bf16[1,384,512]{2,1,0:T(8,128)(2,1)S(1)} %get-tuple-element.551), channel_id=1, source_target_pairs={{0,8},{1,9},{2,10},{3,11},{4,12},{5,13},{6,14},{7,15},{8,0},{9,1},... | collective-permute-start | bytes 1179656 | tf_op jit(solution)/shard_map/cond/branch_1_fun/ppermute | solution.py:636
  300.1 31.0 %collective-permute-start.44 = (bf16[1,208,512]{2,1,0:T(8,128)(2,1)S(1)}, bf16[1,208,512]{2,1,0:T(8,128)(2,1)S(1)}, u32[]{:S(2)}, u32[]{:S(2)}) collective-permute-start(bf16[1,208,512]{2,1,0:T(8,128)(2,1)S(1)} %get-tuple-element.554), channel_id=1, source_target_pairs={{0,8},{1,9},{2,10},{3,11},{4,12},{5,13},{6,14},{7,15},{8,0},{9,1},... | collective-permute-start | bytes 638984 | tf_op jit(solution)/shard_map/cond/branch_1_fun/ppermute | solution.py:636
  301.2 30.0 %collective-permute-start.45 = (bf16[1,208,512]{2,1,0:T(8,128)(2,1)S(1)}, bf16[1,208,512]{2,1,0:T(8,128)(2,1)S(1)}, u32[]{:S(2)}, u32[]{:S(2)}) collective-permute-start(bf16[1,208,512]{2,1,0:T(8,128)(2,1)S(1)} %get-tuple-element.558), channel_id=1, source_target_pairs={{0,8},{1,9},{2,10},{3,11},{4,12},{5,13},{6,14},{7,15},{8,0},{9,1},... | collective-permute-start | bytes 638984 | tf_op jit(solution)/shard_map/cond/branch_1_fun/ppermute | solution.py:636
  (37 other events, 336.8 us)
where the time goes:
time: 339 us; the launch traced here: 334 us
  waiting for transfers between devices  157 us (46%)
  Pallas kernels  123 us (36%)
  starting transfers between devices  36.8 us (11%)
  loops' own time  9.95 us (3%)
    ppermute x23, waiting for transfers between devices, swap(): return lax.ppermute(block, 'dp', [(i, i ^ 1 << bit) for i in range(count)])  90.8 us
    ppermute x1, waiting for transfers between devices, local(): received = lax.ppermute(delta, 'section', [(1, 0)])  62.7 us
    pallas_call x1, Pallas kernels, forward(): pl.pallas_call(functools.partial(forward_kernel, rows, with_delta, orders...  28.8 us
    ppermute x23, starting transfers between devices, swap(): return lax.ppermute(block, 'dp', [(i, i ^ 1 << bit) for i in range(count)])  25.8 us
    pallas_call x1, Pallas kernels, channel(): pl.pallas_call(functools.partial(channel_kernel, rows, times), out_shape=...  21.8 us
    pallas_call x2, Pallas kernels, terms(): pl.pallas_call(functools.partial(terms_kernel, count, parts, shapes, bool...  21.3 us
    pallas_call x1, Pallas kernels, time_mix(): pl.pallas_call(functools.partial(time_kernel, rows), out_shape=tuple((jax...  21.3 us
    pallas_call x14, Pallas kernels, advance(): pl.pallas_call(advance_kernel, out_shape=(jax.ShapeDtypeStruct((half, row...  17.1 us
  transfers between devices with their start and end apart: 27, of which 13 were waited for; matrix products, arithmetic and copies ran while one was open for 0% of the time, Pallas kernels for 28%

commit v1 on v0

--- a/solution.py
+++ b/solution.py
@@ -857,18 +857,18 @@
 
 VECTORS = (0, 1, 5, 6, 2, 3, 4, 8, 9, 10, 11)
 PARTS_0 = dict(
-    a=((512, (2, 1, 0, 3)), (512, (1, 2, 0, 3))),
-    b=((512, (1, 2, 0, 3)), (512, (0, 1, 2, 3))),
-    e=((512, (2, 0, 1, 3)), (512, (1, 0, 2, 3))),
+    a=((512, (0, 1, 2, 3)), (512, (2, 1, 0, 3))),
+    b=((512, (2, 1, 0, 3)), (512, (0, 1, 2, 3))),
+    e=((512, (1, 0, 2, 3)), (512, (0, 2, 1, 3))),
 )
 PARTS_1 = dict(
-    a=((512, (1, 2, 0, 3)), (512, (2, 1, 0, 3))),
-    b=((512, (2, 0, 1, 3)), (512, (0, 2, 1, 3))),
+    a=((512, (1, 0, 2, 3)), (512, (2, 0, 1, 3))),
+    b=((512, (1, 0, 2, 3)), (512, (2, 0, 1, 3))),
     e=((512, (1, 0, 2, 3)), (512, (2, 0, 1, 3))),
 )
-ORDER_1 = ('a', 'b', 'e')
-STEPS_0 = (('a', 1, 2), ('b', 0, 1), ('a', 0, 2), ('b', 1, 1), ('e', 1, 1), ('e', 0, 1), ('a', 0, 3), ('b', 1, 2), ('b', 0, 2), ('e', 1, 2), ('a', 0, 4), ('e', 0, 2), ('b', 1, 3), ('b', 0, 3), ('e', 0, 3), ('e', 1, 3), ('b', 1, 4), ('b', 0, 4), ('e', 0, 4), ('e', 1, 4))
-STEPS_1 = (('a', 0, 2), ('a', 1, 2), ('b', 0, 1), ('e', 0, 1), ('b', 1, 1), ('e', 1, 1), ('a', 0, 3), ('b', 1, 2), ('b', 0, 2), ('a', 0, 4), ('b', 1, 3), ('b', 0, 3), ('e', 0, 2), ('b', 1, 4), ('b', 0, 4), ('e', 1, 2), ('e', 0, 3), ('e', 1, 3), ('e', 0, 4), ('e', 1, 4))
+ORDER_1 = ('b', 'a', 'e')
+STEPS_0 = (('a', 0, 2), ('a', 1, 2), ('b', 1, 1), ('b', 0, 1), ('e', 0, 1), ('b', 1, 2), ('e', 1, 1), ('a', 0, 3), ('b', 1, 3), ('b', 0, 2), ('e', 1, 2), ('e', 0, 2), ('a', 0, 4), ('b', 0, 3), ('b', 1, 4), ('e', 0, 3), ('e', 1, 3), ('b', 0, 4), ('e', 0, 4), ('e', 1, 4))
+STEPS_1 = (('a', 0, 2), ('a', 1, 2), ('b', 0, 1), ('b', 1, 1), ('e', 0, 1), ('b', 0, 2), ('e', 1, 1), ('a', 0, 3), ('b', 0, 3), ('b', 1, 2), ('a', 0, 4), ('b', 0, 4), ('e', 0, 2), ('b', 1, 3), ('e', 0, 3), ('e', 1, 2), ('b', 1, 4), ('e', 1, 3), ('e', 0, 4), ('e', 1, 4))
 
 
 def local(entry_pair, labels, *params):

time: 339 us -> 332 us (0.979)
  waiting for transfers between devices: 157 us -> 152 us
    ppermute x23, waiting for transfers between devices: 90.8 us -> 86.4 us  [swap(): return lax.ppermute(block, 'dp', [(i, i ^ 1 << bit) for i in range(count)])]
  transfers between devices with their start and end apart: 27 -> 27, of which waited for: 13 -> 13; matrix products, arithmetic and copies ran while one was open for 0% -> 0% of each run, Pallas kernels for 28% -> 29%
where the time goes in v1:
time: 332 us; the launch traced here: 327 us
  waiting for transfers between devices  152 us (46%)
  Pallas kernels  124 us (37%)
  starting transfers between devices  33.9 us (10%)
  loops' own time  9.9 us (3%)
    ppermute x23, waiting for transfers between devices, swap(): return lax.ppermute(block, 'dp', [(i, i ^ 1 << bit) for i in range(count)])  86.4 us
    ppermute x1, waiting for transfers between devices, local(): received = lax.ppermute(delta, 'section', [(1, 0)])  62.8 us
    pallas_call x1, Pallas kernels, forward(): pl.pallas_call(functools.partial(forward_kernel, rows, with_delta, orders...  28.8 us
    ppermute x23, starting transfers between devices, swap(): return lax.ppermute(block, 'dp', [(i, i ^ 1 << bit) for i in range(count)])  22.9 us
    pallas_call x1, Pallas kernels, channel(): pl.pallas_call(functools.partial(channel_kernel, rows, times), out_shape=...  21.8 us
    pallas_call x2, Pallas kernels, terms(): pl.pallas_call(functools.partial(terms_kernel, count, parts, shapes, bool...  21.4 us
    pallas_call x1, Pallas kernels, time_mix(): pl.pallas_call(functools.partial(time_kernel, rows), out_shape=tuple((jax...  21.3 us
    pallas_call x14, Pallas kernels, advance(): pl.pallas_call(advance_kernel, out_shape=(jax.ShapeDtypeStruct((half, row...  17.4 us
  transfers between devices with their start and end apart: 27, of which 13 were waited for; matrix products, arithmetic and copies ran while one was open for 0% of the time, Pallas kernels for 29%

profile of v1, /device:TPU:0, one launch (start us, length us, event | category | flops | bytes accessed | tf_op | source)
XLA Modules:
  0.0 327.2 jit_solution(12980840878918395742)
XLA Ops:
  1.8 28.8 %conditional.3 = ((bf16[512,1024]{1,0:T(8,128)(2,1)}, bf16[512,1024]{1,0:T(8,128)(2,1)}, bf16[512,1024]{1,0:T(8,128)(2,1)}, f32[4096,128]{1,0:T(8,128)}, f32[409...) conditional(s32[]{:T(128)} %convert_element_type.18, () %tuple.78, ...), branch_computations={%region_0.0_spmd, %region_1.0_spmd} | conditional | flops 89999998976 | bytes 261000000 | solution.py:959
  1.8 28.8 %forward.2 = (bf16[512,1024]{1,0:T(8,128)(2,1)}, bf16[512,1024]{1,0:T(8,128)(2,1)}, bf16[512,1024]{1,0:T(8,128)(2,1)}, f32[4096,128]{1,0:T(8,128)}, f32[4096,128...) custom-call(s32[4]{0:T(128)S(1)} %get-tuple-element.226.refs_0_, ...), custom_call_target="tpu_custom_call" | custom-call | flops 89999998976 | bytes 261000000 | tf_op jit(solution)/shard_map/cond/branch_1_fun/forward/pallas_call | solution.py:239
  32.0 4.9 %collective-permute-start.48 = (bf16[512,1024]{1,0:T(8,128)(2,1)}, bf16[512,1024]{1,0:T(8,128)(2,1)}, u32[]{:S(2)}, u32[]{:S(2)}) collective-permute-start(bf16[512,1024]{1,0:T(8,128)(2,1)} %get-tuple-element.694), channel_id=1, source_target_pairs={{0,1},{1,0},{2,3},{3,2},{4,5},{5,4},{6,7},{7,6},{8,9},{9,8},{10,11... | collective-permute-start | bytes 3145736 | tf_op jit(solution)/shard_map/ppermute | solution.py:957
  36.8 3.5 %collective-permute-start.49 = (bf16[512,1024]{1,0:T(8,128)(2,1)}, bf16[512,1024]{1,0:T(8,128)(2,1)}, u32[]{:S(2)}, u32[]{:S(2)}) collective-permute-start(bf16[512,1024]{1,0:T(8,128)(2,1)} %get-tuple-element.696), channel_id=1, source_target_pairs={{0,4},{1,5},{2,6},{3,7},{4,0},{5,1},{6,2},{7,3},{8,12},{9,13},{10,... | collective-permute-start | bytes 3145736 | tf_op jit(solution)/shard_map/ppermute | solution.py:957
  40.3 9.1 %conditional.4 = ((bf16[512,1024]{1,0:T(8,128)(2,1)}, bf16[512,1024]{1,0:T(8,128)(2,1)}, bf16[512,1024]{1,0:T(8,128)(2,1)}, bf16[512,1024]{1,0:T(8,128)(2,1)}, b...) conditional(s32[]{:T(128)} %convert_element_type.19, () %tuple.77, ...), branch_computations={%region_2.0_spmd, %region_3.0_spmd} | conditional | flops 251999977472 | bytes 764445248 | solution.py:962
  50.7 3.1 collective-permute-done.49
  53.8 62.8 %collective-permute-done.47 = bf16[512,1024]{1,0:T(8,128)(2,1)} collective-permute-done((bf16[512,1024]{1,0:T(8,128)(2,1)}, bf16[512,1024]{1,0:T(8,128)(2,1)}, u32[]{:S(2)}, u32[]{:S(2)}) %collective-permute-start.47) | collective-permute-done | bytes 1048608 | tf_op jit(solution)/shard_map/ppermute | solution.py:963
  116.6 209.3 %conditional.5 = (f32[64,4096]{1,0:T(8,128)}, f32[64,1024]{1,0:T(8,128)}, f32[64,1024]{1,0:T(8,128)}, f32[64,1024]{1,0:T(8,128)}, f32[64,1024]{1,0:T(8,128)}, /*...) conditional(s32[]{:T(128)} %convert_element_type.18, ...), branch_computations={%region_4.0_spmd, %region_5.0_spmd} | conditional | flops 414001987584 | bytes 1378309504 | solution.py:964
  121.4 21.8 %channel.3 = (bf16[512,4096]{1,0:T(8,128)(2,1)}, f32[512,1024]{1,0:T(8,128)}, bf16[512,1024]{1,0:T(8,128)(2,1)}, f32[8,1024]{1,0:T(8,128)}, bf16[512,1024]{1,0:T(8,128)(2,1)}, /*index=5*/bf16[512,1024]{1,0:T(8,128)(2,1)}) custom-call(f32[512,128]{1,0:T(8,128)S(1)} %copy-done.16, bf16[512,1024]{1,0:T(8,128)(2,1)S(1)} %copy-done.13, ...), custom_call_target="tpu_custom_call" | custom-call | flops 74999996416 | bytes 217500000 | tf_op jit(solution)/shard_map/cond/branch_1_fun/channel/pallas_call | solution.py:374
  143.3 12.7 %terms.6 = (bf16[8,384,512]{2,1,0:T(8,128)(2,1)}, bf16[8,384,512]{2,1,0:T(8,128)(2,1)}, bf16[8,384,512]{2,1,0:T(8,128)(2,1)}, bf16[8,384,512]{2,1,0:T(8,128)(2,1)}) custom-call(s32[4]{0:T(128)S(1)} %copy-done.22, bf16[512,1024]{1,0:T(8,128)(2,1)} %get-tuple-element.442.refs_1_, bf16[512,1024]{1,0:T(8,128)(2,1)} %get-tuple-element.443.refs_2_, ...), custom_call_target="tpu_custom_call" | custom-call | flops 38999998464 | bytes 113100000 | tf_op jit(solution)/shard_map/cond/branch_1_fun/terms/pallas_call | solution.py:620
  159.3 9.8 %values.3 = (bf16[2,256,1024]{2,1,0:T(8,128)(2,1)}, bf16[2,256,1024]{2,1,0:T(8,128)(2,1)}, bf16[2,256,1024]{2,1,0:T(8,128)(2,1)}, bf16[2,256,1024]{2,1,0:T(8,128)(2,1)}) custom-call(s32[4]{0:T(128)S(1)} %copy-done.22, bf16[512,1024]{1,0:T(8,128)(2,1)} %copy-done.12, bf16[512,1024]{1,0:T(8,128)(2,1)S(1)} %copy-done.51, ...), custom_call_target="tpu_custom_call" | custom-call | flops 30000001024 | bytes 87000000 | tf_op jit(solution)/shard_map/cond/branch_1_fun/values/pallas_call | solution.py:749
  171.3 21.3 %time_mix.3 = (bf16[512,1024]{1,0:T(8,128)(2,1)}, bf16[512,1024]{1,0:T(8,128)(2,1)}, bf16[512,1024]{1,0:T(8,128)(2,1)}, f32[512,1024]{1,0:T(8,128)}, f32[8,1024]{1,0:T(8,128)}) custom-call(f32[2,256]{1,0:T(2,128)S(1)} %copy-done.18, f32[512,128]{1,0:T(8,128)S(1)} %copy-done.16, bf16[512,1024]{1,0:T(8,128)(2,1)} %get-tuple-element.462.refs_6_.refs_2_, ...), custom_call_target="tpu_custom_call" | custom-call | flops 86999998464 | bytes 252300000 | tf_op jit(solution)/shard_map/cond/branch_1_fun/time_mix/pallas_call | solution.py:491
  192.6 8.6 %terms.7 = (bf16[8,208,512]{2,1,0:T(8,128)(2,1)}, bf16[8,208,512]{2,1,0:T(8,128)(2,1)}, bf16[8,208,512]{2,1,0:T(8,128)(2,1)}, bf16[8,208,512]{2,1,0:T(8,128)(2,1)}) custom-call(s32[4]{0:T(128)S(1)} %copy-done.22, bf16[512,1024]{1,0:T(8,128)(2,1)} %get-tuple-element.484.refs_1_, bf16[512,1024]{1,0:T(8,128)(2,1)} %get-tuple-element.485.refs_2_, ...), custom_call_target="tpu_custom_call" | custom-call | flops 38999998464 | bytes 113100000 | tf_op jit(solution)/shard_map/cond/branch_1_fun/terms/pallas_call | solution.py:620
  201.8 10.5 %collective-permute-done.28.came_go.came_stay = bf16[2,256,1024]{2,1,0:T(8,128)(2,1)S(1)} collective-permute-done((bf16[2,256,1024]{2,1,0:T(8,128)(2,1)}, bf16[2,256,1024]{2,1,0:T(8,128)(2,1)S(1)}, u32[]{:S(2)}, u32[]{:S(2)}) %collective-permute-start.28) | collective-permute-done | bytes 1048608 | tf_op jit(solution)/shard_map/cond/branch_1_fun/ppermute | solution.py:636
  217.0 3.9 %advance.44 = (bf16[4,384,512]{2,1,0:T(8,128)(2,1)S(1)}, bf16[4,384,512]{2,1,0:T(8,128)(2,1)S(1)}) custom-call(s32[4]{0:T(128)S(1)} %copy-done.22, bf16[8,384,512]{2,1,0:T(8,128)(2,1)S(1)} %copy-done.1, bf16[8,384,512]{2,1,0:T(8,128)(2,1)} %collective-permute-done.24.came_go.came_stay, bf16[8,384,512]{2,1,0:T(8,128)(2,1)S(1)} %copy-done.1, ...), custom_call_target="tpu_custom_call" | custom-call | flops 8999999488 | bytes 26100000 | tf_op jit(solution)/shard_map/cond/branch_1_fun/advance/pallas_call | solution.py:655
  220.9 6.5 %collective-permute-done.23.came_go.came_stay = bf16[8,384,512]{2,1,0:T(8,128)(2,1)} collective-permute-done((bf16[8,384,512]{2,1,0:T(8,128)(2,1)}, bf16[8,384,512]{2,1,0:T(8,128)(2,1)}, u32[]{:S(2)}, u32[]{:S(2)}) %collective-permute-start.23) | collective-permute-done | bytes 3145760 | tf_op jit(solution)/shard_map/cond/branch_1_fun/ppermute | solution.py:636
  228.0 3.6 %advance.45 = (bf16[4,384,512]{2,1,0:T(8,128)(2,1)S(1)}, bf16[4,384,512]{2,1,0:T(8,128)(2,1)S(1)}) custom-call(s32[4]{0:T(128)S(1)} %copy-done.22, bf16[8,384,512]{2,1,0:T(8,128)(2,1)S(1)} %copy-done, bf16[8,384,512]{2,1,0:T(8,128)(2,1)} %collective-permute-done.23.came_go.came_stay, bf16[8,384,512]{2,1,0:T(8,128)(2,1)S(1)} %copy-done, ...), custom_call_target="tpu_custom_call" | custom-call | flops 8999999488 | bytes 26100000 | tf_op jit(solution)/shard_map/cond/branch_1_fun/advance/pallas_call | solution.py:655
  234.3 13.6 %collective-permute-done.30.came_go.came_stay = bf16[4,384,512]{2,1,0:T(8,128)(2,1)S(1)} collective-permute-done((bf16[4,384,512]{2,1,0:T(8,128)(2,1)S(1)}, bf16[4,384,512]{2,1,0:T(8,128)(2,1)S(1)}, u32[]{:S(2)}, u32[]{:S(2)}) %collective-permute-start.30) | collective-permute-done | bytes 1572896 | tf_op jit(solution)/shard_map/cond/branch_1_fun/ppermute | solution.py:636
  254.1 9.7 %collective-permute-done.34.came_b = bf16[1,256,1024]{2,1,0:T(8,128)(2,1)S(1)} collective-permute-done((bf16[1,256,1024]{2,1,0:T(8,128)(2,1)S(1)}, bf16[1,256,1024]{2,1,0:T(8,128)(2,1)S(1)}, u32[]{:S(2)}, u32[]{:S(2)}) %collective-permute-start.34) | collective-permute-done | bytes 524320 | tf_op jit(solution)/shard_map/cond/branch_1_fun/ppermute | solution.py:636
  269.2 4.0 %collective-permute-done.29.came_go.came_stay = bf16[4,384,512]{2,1,0:T(8,128)(2,1)S(1)} collective-permute-done((bf16[4,384,512]{2,1,0:T(8,128)(2,1)S(1)}, bf16[4,384,512]{2,1,0:T(8,128)(2,1)S(1)}, u32[]{:S(2)}, u32[]{:S(2)}) %collective-permute-start.29) | collective-permute-done | bytes 1572896 | tf_op jit(solution)/shard_map/cond/branch_1_fun/ppermute | solution.py:636
  275.2 19.2 %collective-permute-done.39.came_go.came_stay = bf16[4,208,512]{2,1,0:T(8,128)(2,1)S(1)} collective-permute-done((bf16[4,208,512]{2,1,0:T(8,128)(2,1)S(1)}, bf16[4,208,512]{2,1,0:T(8,128)(2,1)S(1)}, u32[]{:S(2)}, u32[]{:S(2)}) %collective-permute-start.39) | collective-permute-done | bytes 852000 | tf_op jit(solution)/shard_map/cond/branch_1_fun/ppermute | solution.py:636
  299.2 9.5 %collective-permute-done.41.came_go.came_stay = bf16[2,208,512]{2,1,0:T(8,128)(2,1)S(1)} collective-permute-done((bf16[2,208,512]{2,1,0:T(8,128)(2,1)S(1)}, bf16[2,208,512]{2,1,0:T(8,128)(2,1)S(1)}, u32[]{:S(2)}, u32[]{:S(2)}) %collective-permute-start.41) | collective-permute-done | bytes 426016 | tf_op jit(solution)/shard_map/cond/branch_1_fun/ppermute | solution.py:636
  310.1 3.0 collective-permute-start.45
  313.1 7.1 %collective-permute-done.42.refs_1_ = bf16[1,384,512]{2,1,0:T(8,128)(2,1)S(1)} collective-permute-done((bf16[1,384,512]{2,1,0:T(8,128)(2,1)S(1)}, bf16[1,384,512]{2,1,0:T(8,128)(2,1)S(1)}, u32[]{:S(2)}, u32[]{:S(2)}) %collective-permute-start.42) | collective-permute-done | bytes 393248 | tf_op jit(solution)/shard_map/cond/branch_1_fun/ppermute | solution.py:636
  (132 shorter events, 48.2 us)
Async XLA Ops:
  32.0 18.7 %collective-permute-start.48 = (bf16[512,1024]{1,0:T(8,128)(2,1)}, bf16[512,1024]{1,0:T(8,128)(2,1)}, u32[]{:S(2)}, u32[]{:S(2)}) collective-permute-start(bf16[512,1024]{1,0:T(8,128)(2,1)} %get-tuple-element.694), channel_id=1, source_target_pairs={{0,1},{1,0},{2,3},{3,2},{4,5},{5,4},{6,7},{7,6},{8,9},{9,8},{10,11... | collective-permute-start | bytes 3145736 | tf_op jit(solution)/shard_map/ppermute | solution.py:957
  36.8 17.0 %collective-permute-start.49 = (bf16[512,1024]{1,0:T(8,128)(2,1)}, bf16[512,1024]{1,0:T(8,128)(2,1)}, u32[]{:S(2)}, u32[]{:S(2)}) collective-permute-start(bf16[512,1024]{1,0:T(8,128)(2,1)} %get-tuple-element.696), channel_id=1, source_target_pairs={{0,4},{1,5},{2,6},{3,7},{4,0},{5,1},{6,2},{7,3},{8,12},{9,13},{10,... | collective-permute-start | bytes 3145736 | tf_op jit(solution)/shard_map/ppermute | solution.py:957
  49.4 67.3 %collective-permute-start.47 = (bf16[512,1024]{1,0:T(8,128)(2,1)}, bf16[512,1024]{1,0:T(8,128)(2,1)}, u32[]{:S(2)}, u32[]{:S(2)}) collective-permute-start(bf16[512,1024]{1,0:T(8,128)(2,1)} %get-tuple-element.683), channel_id=1, source_target_pairs={{16,0},{17,1},{18,2},{19,3},{20,4},{21,5},{22,6},{23,7},{24,8},{25... | collective-permute-start | bytes 3145736 | tf_op jit(solution)/shard_map/ppermute | solution.py:963
  119.4 38.9 %collective-permute-start.26 = (bf16[512,1024]{1,0:T(8,128)(2,1)S(1)}, bf16[512,1024]{1,0:T(8,128)(2,1)S(1)}, u32[]{:S(2)}, u32[]{:S(2)}) collective-permute-start(bf16[512,1024]{1,0:T(8,128)(2,1)S(1)} %multiply_convert_fusion.own), channel_id=1, source_target_pairs={{0,4},{1,5},{2,6},{3,7},{4,0},{5,1},{6,2},{7,3},{8,12},{9,13},{10,... | collective-permute-start | bytes 3145736 | tf_op jit(solution)/shard_map/cond/branch_1_fun/ppermute | solution.py:636
  119.9 38.3 %collective-permute-start.25 = (bf16[512,1024]{1,0:T(8,128)(2,1)S(1)}, bf16[512,1024]{1,0:T(8,128)(2,1)}, u32[]{:S(2)}, u32[]{:S(2)}) collective-permute-start(bf16[512,1024]{1,0:T(8,128)(2,1)S(1)} %multiply_convert_fusion.own), channel_id=1, source_target_pairs={{0,1},{1,0},{2,3},{3,2},{4,5},{5,4},{6,7},{7,6},{8,9},{9,8},{10,11... | collective-permute-start | bytes 3145736 | tf_op jit(solution)/shard_map/cond/branch_1_fun/ppermute | solution.py:636
  156.1 71.4 %collective-permute-start.23 = (bf16[8,384,512]{2,1,0:T(8,128)(2,1)}, bf16[8,384,512]{2,1,0:T(8,128)(2,1)}, u32[]{:S(2)}, u32[]{:S(2)}) collective-permute-start(bf16[8,384,512]{2,1,0:T(8,128)(2,1)} %get-tuple-element.448), channel_id=1, source_target_pairs={{0,4},{1,5},{2,6},{3,7},{4,0},{5,1},{6,2},{7,3},{8,12},{9,13},{10,... | collective-permute-start | bytes 9437192 | tf_op jit(solution)/shard_map/cond/branch_1_fun/ppermute | solution.py:636
  157.7 58.2 %collective-permute-start.24 = (bf16[8,384,512]{2,1,0:T(8,128)(2,1)}, bf16[8,384,512]{2,1,0:T(8,128)(2,1)}, u32[]{:S(2)}, u32[]{:S(2)}) collective-permute-start(bf16[8,384,512]{2,1,0:T(8,128)(2,1)} %get-tuple-element.450), channel_id=1, source_target_pairs={{0,1},{1,0},{2,3},{3,2},{4,5},{5,4},{6,7},{7,6},{8,9},{9,8},{10,11... | collective-permute-start | bytes 9437192 | tf_op jit(solution)/shard_map/cond/branch_1_fun/ppermute | solution.py:636
  169.1 45.5 %collective-permute-start.27 = (bf16[2,256,1024]{2,1,0:T(8,128)(2,1)}, bf16[2,256,1024]{2,1,0:T(8,128)(2,1)S(1)}, u32[]{:S(2)}, u32[]{:S(2)}) collective-permute-start(bf16[2,256,1024]{2,1,0:T(8,128)(2,1)} %get-tuple-element.457), channel_id=1, source_target_pairs={{0,2},{1,3},{2,0},{3,1},{4,6},{5,7},{6,4},{7,5},{8,10},{9,11},{10,... | collective-permute-start | bytes 3145736 | tf_op jit(solution)/shard_map/cond/branch_1_fun/ppermute | solution.py:636
  169.7 42.6 %collective-permute-start.28 = (bf16[2,256,1024]{2,1,0:T(8,128)(2,1)}, bf16[2,256,1024]{2,1,0:T(8,128)(2,1)S(1)}, u32[]{:S(2)}, u32[]{:S(2)}) collective-permute-start(bf16[2,256,1024]{2,1,0:T(8,128)(2,1)} %get-tuple-element.459), channel_id=1, source_target_pairs={{0,2},{1,3},{2,0},{3,1},{4,6},{5,7},{6,4},{7,5},{8,10},{9,11},{10,... | collective-permute-start | bytes 3145736 | tf_op jit(solution)/shard_map/cond/branch_1_fun/ppermute | solution.py:636
  201.2 30.4 %collective-permute-start.31 = (bf16[8,208,512]{2,1,0:T(8,128)(2,1)}, bf16[8,208,512]{2,1,0:T(8,128)(2,1)S(1)}, u32[]{:S(2)}, u32[]{:S(2)}) collective-permute-start(bf16[8,208,512]{2,1,0:T(8,128)(2,1)} %get-tuple-element.492), channel_id=1, source_target_pairs={{0,2},{1,3},{2,0},{3,1},{4,6},{5,7},{6,4},{7,5},{8,10},{9,11},{10,... | collective-permute-start | bytes 5111816 | tf_op jit(solution)/shard_map/cond/branch_1_fun/ppermute | solution.py:636
  212.3 40.4 %collective-permute-start.35 = (bf16[8,208,512]{2,1,0:T(8,128)(2,1)}, bf16[8,208,512]{2,1,0:T(8,128)(2,1)S(1)}, u32[]{:S(2)}, u32[]{:S(2)}) collective-permute-start(bf16[8,208,512]{2,1,0:T(8,128)(2,1)} %get-tuple-element.494), channel_id=1, source_target_pairs={{0,1},{1,0},{2,3},{3,2},{4,5},{5,4},{6,7},{7,6},{8,9},{9,8},{10,11... | collective-permute-start | bytes 5111816 | tf_op jit(solution)/shard_map/cond/branch_1_fun/ppermute | solution.py:636
  214.6 49.7 %collective-permute-start.33 = (bf16[1,256,1024]{2,1,0:T(8,128)(2,1)S(1)}, bf16[1,256,1024]{2,1,0:T(8,128)(2,1)S(1)}, u32[]{:S(2)}, u32[]{:S(2)}) collective-permute-start(bf16[1,256,1024]{2,1,0:T(8,128)(2,1)S(1)} %get-tuple-element.498), channel_id=1, source_target_pairs={{0,4},{1,5},{2,6},{3,7},{4,0},{5,1},{6,2},{7,3},{8,12},{9,13},{10,... | collective-permute-start | bytes 1572872 | tf_op jit(solution)/shard_map/cond/branch_1_fun/ppermute | solution.py:636
  215.9 48.0 %collective-permute-start.34 = (bf16[1,256,1024]{2,1,0:T(8,128)(2,1)S(1)}, bf16[1,256,1024]{2,1,0:T(8,128)(2,1)S(1)}, u32[]{:S(2)}, u32[]{:S(2)}) collective-permute-start(bf16[1,256,1024]{2,1,0:T(8,128)(2,1)S(1)} %get-tuple-element.502), channel_id=1, source_target_pairs={{0,1},{1,0},{2,3},{3,2},{4,5},{5,4},{6,7},{7,6},{8,9},{9,8},{10,11... | collective-permute-start | bytes 1572872 | tf_op jit(solution)/shard_map/cond/branch_1_fun/ppermute | solution.py:636
  227.5 20.4 %collective-permute-start.30 = (bf16[4,384,512]{2,1,0:T(8,128)(2,1)S(1)}, bf16[4,384,512]{2,1,0:T(8,128)(2,1)S(1)}, u32[]{:S(2)}, u32[]{:S(2)}) collective-permute-start(bf16[4,384,512]{2,1,0:T(8,128)(2,1)S(1)} %get-tuple-element.506), channel_id=1, source_target_pairs={{0,2},{1,3},{2,0},{3,1},{4,6},{5,7},{6,4},{7,5},{8,10},{9,11},{10,... | collective-permute-start | bytes 4718600 | tf_op jit(solution)/shard_map/cond/branch_1_fun/ppermute | solution.py:636
  231.7 41.5 %collective-permute-start.29 = (bf16[4,384,512]{2,1,0:T(8,128)(2,1)S(1)}, bf16[4,384,512]{2,1,0:T(8,128)(2,1)S(1)}, u32[]{:S(2)}, u32[]{:S(2)}) collective-permute-start(bf16[4,384,512]{2,1,0:T(8,128)(2,1)S(1)} %get-tuple-element.511), channel_id=1, source_target_pairs={{0,2},{1,3},{2,0},{3,1},{4,6},{5,7},{6,4},{7,5},{8,10},{9,11},{10,... | collective-permute-start | bytes 4718600 | tf_op jit(solution)/shard_map/cond/branch_1_fun/ppermute | solution.py:636
  247.9 47.5 %collective-permute-start.38 = (bf16[4,208,512]{2,1,0:T(8,128)(2,1)S(1)}, bf16[4,208,512]{2,1,0:T(8,128)(2,1)S(1)}, u32[]{:S(2)}, u32[]{:S(2)}) collective-permute-start(bf16[4,208,512]{2,1,0:T(8,128)(2,1)S(1)} %get-tuple-element.514), channel_id=1, source_target_pairs={{0,1},{1,0},{2,3},{3,2},{4,5},{5,4},{6,7},{7,6},{8,9},{9,8},{10,11... | collective-permute-start | bytes 2555912 | tf_op jit(solution)/shard_map/cond/branch_1_fun/ppermute | solution.py:636
  252.7 15.4 %collective-permute-start.32 = (bf16[2,384,512]{2,1,0:T(8,128)(2,1)S(1)}, bf16[2,384,512]{2,1,0:T(8,128)(2,1)S(1)}, u32[]{:S(2)}, u32[]{:S(2)}) collective-permute-start(bf16[2,384,512]{2,1,0:T(8,128)(2,1)S(1)} %get-tuple-element.519), channel_id=1, source_target_pairs={{0,4},{1,5},{2,6},{3,7},{4,0},{5,1},{6,2},{7,3},{8,12},{9,13},{10,... | collective-permute-start | bytes 2359304 | tf_op jit(solution)/shard_map/cond/branch_1_fun/ppermute | solution.py:636
  263.9 30.6 %collective-permute-start.39 = (bf16[4,208,512]{2,1,0:T(8,128)(2,1)S(1)}, bf16[4,208,512]{2,1,0:T(8,128)(2,1)S(1)}, u32[]{:S(2)}, u32[]{:S(2)}) collective-permute-start(bf16[4,208,512]{2,1,0:T(8,128)(2,1)S(1)} %get-tuple-element.522), channel_id=1, source_target_pairs={{0,4},{1,5},{2,6},{3,7},{4,0},{5,1},{6,2},{7,3},{8,12},{9,13},{10,... | collective-permute-start | bytes 2555912 | tf_op jit(solution)/shard_map/cond/branch_1_fun/ppermute | solution.py:636
  265.4 30.9 %collective-permute-start.37 = (bf16[1,256,1024]{2,1,0:T(8,128)(2,1)S(1)}, bf16[1,256,1024]{2,1,0:T(8,128)(2,1)S(1)}, u32[]{:S(2)}, u32[]{:S(2)}) collective-permute-start(bf16[1,256,1024]{2,1,0:T(8,128)(2,1)S(1)} %get-tuple-element.528), channel_id=1, source_target_pairs={{0,8},{1,9},{2,10},{3,11},{4,12},{5,13},{6,14},{7,15},{8,0},{9,1},... | collective-permute-start | bytes 1572872 | tf_op jit(solution)/shard_map/cond/branch_1_fun/ppermute | solution.py:636
  268.8 44.3 %collective-permute-start.43 = (bf16[1,384,512]{2,1,0:T(8,128)(2,1)S(1)}, bf16[1,384,512]{2,1,0:T(8,128)(2,1)S(1)}, u32[]{:S(2)}, u32[]{:S(2)}) collective-permute-start(bf16[1,384,512]{2,1,0:T(8,128)(2,1)S(1)} %get-tuple-element.532), channel_id=1, source_target_pairs={{0,8},{1,9},{2,10},{3,11},{4,12},{5,13},{6,14},{7,15},{8,0},{9,1},... | collective-permute-start | bytes 1179656 | tf_op jit(solution)/shard_map/cond/branch_1_fun/ppermute | solution.py:636
  274.1 22.2 %collective-permute-start.36 = (bf16[2,384,512]{2,1,0:T(8,128)(2,1)S(1)}, bf16[2,384,512]{2,1,0:T(8,128)(2,1)S(1)}, u32[]{:S(2)}, u32[]{:S(2)}) collective-permute-start(bf16[2,384,512]{2,1,0:T(8,128)(2,1)S(1)} %get-tuple-element.537), channel_id=1, source_target_pairs={{0,1},{1,0},{2,3},{3,2},{4,5},{5,4},{6,7},{7,6},{8,9},{9,8},{10,11... | collective-permute-start | bytes 2359304 | tf_op jit(solution)/shard_map/cond/branch_1_fun/ppermute | solution.py:636
  295.3 14.2 %collective-permute-start.40 = (bf16[2,208,512]{2,1,0:T(8,128)(2,1)S(1)}, bf16[2,208,512]{2,1,0:T(8,128)(2,1)S(1)}, u32[]{:S(2)}, u32[]{:S(2)}) collective-permute-start(bf16[2,208,512]{2,1,0:T(8,128)(2,1)S(1)} %get-tuple-element.540), channel_id=1, source_target_pairs={{0,2},{1,3},{2,0},{3,1},{4,6},{5,7},{6,4},{7,5},{8,10},{9,11},{10,... | collective-permute-start | bytes 1277960 | tf_op jit(solution)/shard_map/cond/branch_1_fun/ppermute | solution.py:636
  297.1 23.1 %collective-permute-start.42 = (bf16[1,384,512]{2,1,0:T(8,128)(2,1)S(1)}, bf16[1,384,512]{2,1,0:T(8,128)(2,1)S(1)}, u32[]{:S(2)}, u32[]{:S(2)}) collective-permute-start(bf16[1,384,512]{2,1,0:T(8,128)(2,1)S(1)} %get-tuple-element.551), channel_id=1, source_target_pairs={{0,8},{1,9},{2,10},{3,11},{4,12},{5,13},{6,14},{7,15},{8,0},{9,1},... | collective-permute-start | bytes 1179656 | tf_op jit(solution)/shard_map/cond/branch_1_fun/ppermute | solution.py:636
  310.1 14.6 %collective-permute-start.45 = (bf16[1,208,512]{2,1,0:T(8,128)(2,1)S(1)}, bf16[1,208,512]{2,1,0:T(8,128)(2,1)S(1)}, u32[]{:S(2)}, u32[]{:S(2)}) collective-permute-start(bf16[1,208,512]{2,1,0:T(8,128)(2,1)S(1)} %get-tuple-element.558), channel_id=1, source_target_pairs={{0,8},{1,9},{2,10},{3,11},{4,12},{5,13},{6,14},{7,15},{8,0},{9,1},... | collective-permute-start | bytes 638984 | tf_op jit(solution)/shard_map/cond/branch_1_fun/ppermute | solution.py:636
  (37 other events, 330.9 us)
